TPU v7x, 256 devices: a whole 4x4x8 slice. The times are simulated.
256 devices in a mesh: row: 16 (over z_lo, y, core), col: 16 (over x, z_hi).
Axes of the slice: x: 4, y: 4, z: 8 (z_hi: 4, z_lo: 2; z = z_hi * 2 + z_lo), core: 2. Of those that a mesh axis runs over, the one named last changes fastest.
Arguments:
- positions: float32 [3, 262144], P(None, ('col', 'row')), may hold values from 0 to 16
- velocity: float32 [3, 262144], P(None, ('col', 'row')), may hold values from -6 to 6
- applied: float32 [3, 262144], P(None, ('col', 'row')), may hold values from -12 to 12
- suscept: float32 [262144], P(('col', 'row')), may hold values from 0.05 to 0.3
- contact_owner: int32 [16, 16, 16, 512], P('col', 'row'), may hold values from 0 to 1023
- contact_partner: int32 [16, 16, 16, 512], P('col', 'row'), may hold values from 0 to 1023
- contact_count: int32 [16, 16, 16], P('col', 'row'), may hold values from 1 to 512, as said below
Outputs:
- moments: float32 [3, 262144], P(None, ('col', 'row'))
- forces: float32 [3, 262144], P(None, ('col', 'row'))
Inputs may be any that keep to these rules, and one draw needn't show every extreme that they name: `contact_count`: in every draw one column receives full blocks of 512 live slots from every device; the other columns' blocks are filled to different depths.
All inputs are finite; a program needn't handle non-finite values.
Results may differ from a plain program's by a relative error of at most 0.0003.
Values sent between devices are 32-bit elements; how exact they have to be, the bound alone decides.
A program may use at most 64 MiB of HBM per device.

v0:
```python
import math

import jax
import jax.numpy as jnp
from jax import lax
from jax.sharding import PartitionSpec as P

ITERS = 2


def dipole_block(target_pos, target_ids, source_pos, source_mom, source_ids):
    offset = target_pos[:, :, None] - source_pos[:, None, :]
    radius_sq = jnp.sum(offset * offset, axis=0) + 1.0
    inverse_r = lax.rsqrt(radius_sq)
    inverse_cube = inverse_r * inverse_r * inverse_r
    inverse_fifth = inverse_cube * inverse_r * inverse_r
    keep_mask = target_ids[:, None] != source_ids[None, :]
    projection = jnp.sum(offset * source_mom[:, None, :], axis=0)
    radial_coef = jnp.where(keep_mask, 3.0 * projection * inverse_fifth, 0.0)
    direct_coef = jnp.where(keep_mask, inverse_cube, 0.0)
    return jnp.sum(radial_coef[None] * offset, axis=2) - jnp.sum(
        direct_coef[None] * source_mom[:, None, :], axis=2
    )


def local_field(target_pos, target_ids, source_pos, source_mom, source_ids):
    target_len = target_pos.shape[1]
    source_len = source_pos.shape[1]
    target_block = math.gcd(target_len, 128)
    source_block = math.gcd(source_len, 512)
    target_count = target_len // target_block
    source_count = source_len // source_block
    source_blocks = (
        source_pos.reshape(3, source_count, source_block).transpose(1, 0, 2),
        source_mom.reshape(3, source_count, source_block).transpose(1, 0, 2),
        source_ids.reshape(source_count, source_block),
    )
    target_blocks = (
        target_pos.reshape(3, target_count, target_block).transpose(1, 0, 2),
        target_ids.reshape(target_count, target_block),
    )

    def per_target(target_pair):

        def add_block(field_sum, source_triple):
            return (
                field_sum
                + dipole_block(
                    target_pair[0],
                    target_pair[1],
                    source_triple[0],
                    source_triple[1],
                    source_triple[2],
                ),
                None,
            )

        field_sum, unused = lax.scan(
            add_block, jnp.zeros((3, target_block), jnp.float32), source_blocks
        )
        return field_sum

    result_blocks = lax.map(per_target, target_blocks)
    return result_blocks.transpose(1, 0, 2).reshape(3, target_len)


def pair_force(one_side, other_side):
    separation = one_side[0:3] - other_side[0:3]
    distance = jnp.sqrt(jnp.sum(separation * separation, axis=0) + 1.0)
    normal = separation / distance
    mom_one = one_side[6:9]
    mom_other = other_side[6:9]
    along_one = jnp.sum(mom_one * normal, axis=0)
    along_other = jnp.sum(mom_other * normal, axis=0)
    mom_dot = jnp.sum(mom_one * mom_other, axis=0)
    magnetic = 3.0 * (
        along_one * mom_other
        + along_other * mom_one
        + (mom_dot - 5.0 * along_one * along_other) * normal
    )
    spring = -0.03 * (distance - 1.0) * normal
    rel_speed = jnp.sum((one_side[3:6] - other_side[3:6]) * normal, axis=0)
    damping = -0.5 * rel_speed * normal
    return magnetic + spring + damping


def accumulate(slot_values, slot_ids, particle_count):
    flat_ids = slot_ids.reshape(-1)
    flat_values = slot_values.reshape(3, -1)
    return jnp.zeros((3, particle_count), jnp.float32).at[:, flat_ids].add(flat_values)


def on_device(positions, velocity, applied, suscept, contact_owner, contact_partner, contact_count):
    particle_count = positions.shape[1]
    row_index = lax.axis_index("row")
    own_ids = row_index * particle_count + jnp.arange(particle_count, dtype=jnp.int32)
    moments = suscept[None, :] * applied
    for iteration in range(ITERS):
        shard_pieces = (
            lax.all_gather(positions, "row", axis=1, tiled=True),
            lax.all_gather(moments, "row", axis=1, tiled=True),
        )
        piece_len = shard_pieces[0].shape[1]
        source_ids = jnp.arange(piece_len, dtype=jnp.int32)
        field_sum = local_field(positions, own_ids, shard_pieces[0], shard_pieces[1], source_ids)
        moments = suscept[None, :] * (applied + field_sum)
    col_count = contact_owner.shape[2]
    slot_count = contact_owner.shape[3]
    owner_ids = contact_owner.reshape(col_count, slot_count)
    partner_ids = contact_partner.reshape(col_count, slot_count)
    count_here = contact_count.reshape(col_count)
    live_mask = (jnp.arange(slot_count, dtype=jnp.int32)[None, :] < count_here[:, None]).astype(
        jnp.float32
    )
    state_rows = jnp.concatenate([positions, velocity, moments], axis=0)
    owner_rows = jnp.take(state_rows, owner_ids, axis=1)
    asked_ids = lax.all_to_all(partner_ids, "col", split_axis=0, concat_axis=0, tiled=True)
    looked_up = jnp.take(state_rows, asked_ids, axis=1)
    sent_rows = lax.all_to_all(looked_up, "col", split_axis=1, concat_axis=1, tiled=True)
    partner_rows, asked_ids = (sent_rows, asked_ids[None])
    slot_force = pair_force(owner_rows, partner_rows) * live_mask[None]
    owner_force = accumulate(slot_force, owner_ids, particle_count)
    returned = lax.all_to_all(slot_force, "col", split_axis=1, concat_axis=1, tiled=True)
    forces = owner_force - accumulate(returned, asked_ids[0], particle_count)
    return (moments, forces)


def solution(mesh):
    placed = (
        P(None, ("col", "row")),
        P(None, ("col", "row")),
        P(None, ("col", "row")),
        P(("col", "row")),
        P("col", "row", None, None),
        P("col", "row", None, None),
        P("col", "row", None),
    )
    return jax.shard_map(
        on_device,
        mesh=mesh,
        in_specs=placed,
        out_specs=(P(None, ("col", "row")), P(None, ("col", "row"))),
        check_vma=False,
    )
```

profile of v0, /device:TPU:1, one launch (start us, length us, event | category | flops | bytes accessed | tf_op | source)
XLA Modules:
  0.0 661.3 jit_solution(5421907334864235557)
XLA Ops:
  2.0 11.6 %all-to-all-start = ((s32[16,1,512]{2,1,0:T(1,128)}), s32[16,1,512]{2,1,0:T(1,128)S(1)}, u32[]{:S(2)}, u32[]{:S(2)}) async-start(s32[16,1,512]{2,1,0:T(1,128)} %all_to_all.14), calls=%async_computation | async-start | bytes 65536 | tf_op jit(solution)/shard_map/all_to_all | solution.py:117
  15.2 21.1 %all_gather.10 = f32[3,16384]{1,0:T(4,128)S(1)} all-gather(f32[3,1024]{1,0:T(4,128)} %param.17), channel_id=1, replica_groups=mesh['row'=16,'col'=16] {'row'}, dimensions={1}, use_global_device_ids=true | all-gather | bytes 208896 | tf_op jit(solution)/shard_map/all_gather | solution.py:100
  37.0 17.0 %all_gather.11 = f32[3,16384]{1,0:T(4,128)S(1)} all-gather(f32[3,1024]{1,0:T(4,128)S(1)} %broadcast_multiply_fusion.1), channel_id=1, replica_groups=mesh['row'=16,'col'=16] {'row'}, dimensions={1}, use_global_device_ids=true | all-gather | bytes 208896 | tf_op jit(solution)/shard_map/all_gather | solution.py:101
  54.0 204.9 %while.47 = (s32[]{:T(128)}, f32[8,3,128]{2,1,0:T(4,128)S(1)}, f32[8,3,128]{2,1,0:T(4,128)}, s32[8,128]{1,0:T(8,128)S(1)}, f32[32,3,512]{2,1,0:T(4,128)S(1)}, /*...) while((s32[]{:T(128)}, f32[8,3,128]{2,1,0:T(4,128)S(1)}, ...), condition=%wide.region_7.8_spmd.clone, body=%wide.region_0.7_spmd.clone.sunk | while | flops 2523525 | bytes 2239280 | solution.py:63
  54.7 24.9 %while.50 = (s32[]{:T(128)}, f32[3,128]{1,0:T(4,128)S(1)}, s32[128]{0:T(128)S(1)}, s32[32,512]{1,0:T(8,128)S(1)}, f32[3,128]{1,0:T(4,128)S(1)}, /*index=5*/f32[3...) while((s32[]{:T(128)}, f32[3,128]{1,0:T(4,128)S(1)}, s32[128]{0:T(128)S(1)}, ...), condition=%wide.region_6.6_spmd.clone, body=%wide.region_1.5_spmd.clone.sunk | while | flops 2490755 | bytes 2165359 | solution.py:58
  80.3 24.9 %while.50 = (s32[]{:T(128)}, f32[3,128]{1,0:T(4,128)S(1)}, s32[128]{0:T(128)S(1)}, s32[32,512]{1,0:T(8,128)S(1)}, f32[3,128]{1,0:T(4,128)S(1)}, /*index=5*/f32[3...) while((s32[]{:T(128)}, f32[3,128]{1,0:T(4,128)S(1)}, s32[128]{0:T(128)S(1)}, ...), condition=%wide.region_6.6_spmd.clone, body=%wide.region_1.5_spmd.clone.sunk | while | flops 2490755 | bytes 2165359 | solution.py:58
  105.9 24.9 %while.50 = (s32[]{:T(128)}, f32[3,128]{1,0:T(4,128)S(1)}, s32[128]{0:T(128)S(1)}, s32[32,512]{1,0:T(8,128)S(1)}, f32[3,128]{1,0:T(4,128)S(1)}, /*index=5*/f32[3...) while((s32[]{:T(128)}, f32[3,128]{1,0:T(4,128)S(1)}, s32[128]{0:T(128)S(1)}, ...), condition=%wide.region_6.6_spmd.clone, body=%wide.region_1.5_spmd.clone.sunk | while | flops 2490755 | bytes 2165359 | solution.py:58
  131.5 24.9 %while.50 = (s32[]{:T(128)}, f32[3,128]{1,0:T(4,128)S(1)}, s32[128]{0:T(128)S(1)}, s32[32,512]{1,0:T(8,128)S(1)}, f32[3,128]{1,0:T(4,128)S(1)}, /*index=5*/f32[3...) while((s32[]{:T(128)}, f32[3,128]{1,0:T(4,128)S(1)}, s32[128]{0:T(128)S(1)}, ...), condition=%wide.region_6.6_spmd.clone, body=%wide.region_1.5_spmd.clone.sunk | while | flops 2490755 | bytes 2165359 | solution.py:58
  157.2 24.9 %while.50 = (s32[]{:T(128)}, f32[3,128]{1,0:T(4,128)S(1)}, s32[128]{0:T(128)S(1)}, s32[32,512]{1,0:T(8,128)S(1)}, f32[3,128]{1,0:T(4,128)S(1)}, /*index=5*/f32[3...) while((s32[]{:T(128)}, f32[3,128]{1,0:T(4,128)S(1)}, s32[128]{0:T(128)S(1)}, ...), condition=%wide.region_6.6_spmd.clone, body=%wide.region_1.5_spmd.clone.sunk | while | flops 2490755 | bytes 2165359 | solution.py:58
  182.8 24.9 %while.50 = (s32[]{:T(128)}, f32[3,128]{1,0:T(4,128)S(1)}, s32[128]{0:T(128)S(1)}, s32[32,512]{1,0:T(8,128)S(1)}, f32[3,128]{1,0:T(4,128)S(1)}, /*index=5*/f32[3...) while((s32[]{:T(128)}, f32[3,128]{1,0:T(4,128)S(1)}, s32[128]{0:T(128)S(1)}, ...), condition=%wide.region_6.6_spmd.clone, body=%wide.region_1.5_spmd.clone.sunk | while | flops 2490755 | bytes 2165359 | solution.py:58
  208.4 24.9 %while.50 = (s32[]{:T(128)}, f32[3,128]{1,0:T(4,128)S(1)}, s32[128]{0:T(128)S(1)}, s32[32,512]{1,0:T(8,128)S(1)}, f32[3,128]{1,0:T(4,128)S(1)}, /*index=5*/f32[3...) while((s32[]{:T(128)}, f32[3,128]{1,0:T(4,128)S(1)}, s32[128]{0:T(128)S(1)}, ...), condition=%wide.region_6.6_spmd.clone, body=%wide.region_1.5_spmd.clone.sunk | while | flops 2490755 | bytes 2165359 | solution.py:58
  234.0 24.9 %while.50 = (s32[]{:T(128)}, f32[3,128]{1,0:T(4,128)S(1)}, s32[128]{0:T(128)S(1)}, s32[32,512]{1,0:T(8,128)S(1)}, f32[3,128]{1,0:T(4,128)S(1)}, /*index=5*/f32[3...) while((s32[]{:T(128)}, f32[3,128]{1,0:T(4,128)S(1)}, s32[128]{0:T(128)S(1)}, ...), condition=%wide.region_6.6_spmd.clone, body=%wide.region_1.5_spmd.clone.sunk | while | flops 2490755 | bytes 2165359 | solution.py:58
  258.9 18.3 %all_gather.12 = f32[3,16384]{1,0:T(4,128)S(1)} all-gather(f32[3,1024]{1,0:T(4,128)S(1)} %fusion.26), channel_id=1, replica_groups=mesh['row'=16,'col'=16] {'row'}, dimensions={1}, use_global_device_ids=true | all-gather | bytes 208896 | tf_op jit(solution)/shard_map/all_gather | solution.py:101
  277.2 204.9 %while.49 = (s32[]{:T(128)}, f32[8,3,128]{2,1,0:T(4,128)S(1)}, f32[8,3,128]{2,1,0:T(4,128)}, s32[8,128]{1,0:T(8,128)S(1)}, f32[32,3,512]{2,1,0:T(4,128)S(1)}, /*...) while((s32[]{:T(128)}, f32[8,3,128]{2,1,0:T(4,128)S(1)}, ...), condition=%wide.region_15.16_spmd.clone, body=%wide.region_8.15_spmd.clone.sunk | while | flops 2523525 | bytes 2239280 | solution.py:63
  278.0 24.9 %while.51 = (s32[]{:T(128)}, f32[3,128]{1,0:T(4,128)S(1)}, s32[128]{0:T(128)S(1)}, s32[32,512]{1,0:T(8,128)S(1)}, f32[3,128]{1,0:T(4,128)S(1)}, /*index=5*/f32[3...) while((s32[]{:T(128)}, f32[3,128]{1,0:T(4,128)S(1)}, s32[128]{0:T(128)S(1)}, ...), condition=%wide.region_14.14_spmd.clone, body=%wide.region_9.13_spmd.clone.sunk | while | flops 2490755 | bytes 2165359 | solution.py:58
  303.6 24.9 %while.51 = (s32[]{:T(128)}, f32[3,128]{1,0:T(4,128)S(1)}, s32[128]{0:T(128)S(1)}, s32[32,512]{1,0:T(8,128)S(1)}, f32[3,128]{1,0:T(4,128)S(1)}, /*index=5*/f32[3...) while((s32[]{:T(128)}, f32[3,128]{1,0:T(4,128)S(1)}, s32[128]{0:T(128)S(1)}, ...), condition=%wide.region_14.14_spmd.clone, body=%wide.region_9.13_spmd.clone.sunk | while | flops 2490755 | bytes 2165359 | solution.py:58
  329.2 24.9 %while.51 = (s32[]{:T(128)}, f32[3,128]{1,0:T(4,128)S(1)}, s32[128]{0:T(128)S(1)}, s32[32,512]{1,0:T(8,128)S(1)}, f32[3,128]{1,0:T(4,128)S(1)}, /*index=5*/f32[3...) while((s32[]{:T(128)}, f32[3,128]{1,0:T(4,128)S(1)}, s32[128]{0:T(128)S(1)}, ...), condition=%wide.region_14.14_spmd.clone, body=%wide.region_9.13_spmd.clone.sunk | while | flops 2490755 | bytes 2165359 | solution.py:58
  354.8 24.9 %while.51 = (s32[]{:T(128)}, f32[3,128]{1,0:T(4,128)S(1)}, s32[128]{0:T(128)S(1)}, s32[32,512]{1,0:T(8,128)S(1)}, f32[3,128]{1,0:T(4,128)S(1)}, /*index=5*/f32[3...) while((s32[]{:T(128)}, f32[3,128]{1,0:T(4,128)S(1)}, s32[128]{0:T(128)S(1)}, ...), condition=%wide.region_14.14_spmd.clone, body=%wide.region_9.13_spmd.clone.sunk | while | flops 2490755 | bytes 2165359 | solution.py:58
  380.4 24.9 %while.51 = (s32[]{:T(128)}, f32[3,128]{1,0:T(4,128)S(1)}, s32[128]{0:T(128)S(1)}, s32[32,512]{1,0:T(8,128)S(1)}, f32[3,128]{1,0:T(4,128)S(1)}, /*index=5*/f32[3...) while((s32[]{:T(128)}, f32[3,128]{1,0:T(4,128)S(1)}, s32[128]{0:T(128)S(1)}, ...), condition=%wide.region_14.14_spmd.clone, body=%wide.region_9.13_spmd.clone.sunk | while | flops 2490755 | bytes 2165359 | solution.py:58
  406.0 24.9 %while.51 = (s32[]{:T(128)}, f32[3,128]{1,0:T(4,128)S(1)}, s32[128]{0:T(128)S(1)}, s32[32,512]{1,0:T(8,128)S(1)}, f32[3,128]{1,0:T(4,128)S(1)}, /*index=5*/f32[3...) while((s32[]{:T(128)}, f32[3,128]{1,0:T(4,128)S(1)}, s32[128]{0:T(128)S(1)}, ...), condition=%wide.region_14.14_spmd.clone, body=%wide.region_9.13_spmd.clone.sunk | while | flops 2490755 | bytes 2165359 | solution.py:58
  431.6 24.9 %while.51 = (s32[]{:T(128)}, f32[3,128]{1,0:T(4,128)S(1)}, s32[128]{0:T(128)S(1)}, s32[32,512]{1,0:T(8,128)S(1)}, f32[3,128]{1,0:T(4,128)S(1)}, /*index=5*/f32[3...) while((s32[]{:T(128)}, f32[3,128]{1,0:T(4,128)S(1)}, s32[128]{0:T(128)S(1)}, ...), condition=%wide.region_14.14_spmd.clone, body=%wide.region_9.13_spmd.clone.sunk | while | flops 2490755 | bytes 2165359 | solution.py:58
  457.2 24.9 %while.51 = (s32[]{:T(128)}, f32[3,128]{1,0:T(4,128)S(1)}, s32[128]{0:T(128)S(1)}, s32[32,512]{1,0:T(8,128)S(1)}, f32[3,128]{1,0:T(4,128)S(1)}, /*index=5*/f32[3...) while((s32[]{:T(128)}, f32[3,128]{1,0:T(4,128)S(1)}, s32[128]{0:T(128)S(1)}, ...), condition=%wide.region_14.14_spmd.clone, body=%wide.region_9.13_spmd.clone.sunk | while | flops 2490755 | bytes 2165359 | solution.py:58
  483.3 27.7 %gather_fusion.1 = f32[8192,9]{1,0:T(8,128)} fusion(f32[9,1024]{0,1:T(8,128)S(1)} %copy.38, s32[8192]{0:T(1024)S(1)} %broadcast_clamp_fusion), kind=kCustom, calls=%fused_computation.1.clone | custom fusion | bytes 622592 | tf_op jit(solution)/shard_map/jit(_take)/gather | solution.py:118
  511.0 2.8 copy.41
  514.7 9.5 %all-to-all-start.1 = ((f32[9,16,512]{2,0,1:T(8,128)}), f32[9,16,512]{2,0,1:T(8,128)S(1)}, u32[]{:S(2)}, u32[]{:S(2)}) async-start(f32[9,16,512]{2,0,1:T(8,128)} %select_bitcast_fusion), calls=%async_computation.1 | async-start | bytes 1048576 | tf_op jit(solution)/shard_map/all_to_all | solution.py:119
  524.3 27.7 %gather_fusion = f32[8192,9]{1,0:T(8,128)} fusion(f32[9,1024]{0,1:T(8,128)S(1)} %copy.38, s32[8192]{0:T(1024)S(1)} %broadcast_clamp_fusion.1), kind=kCustom, calls=%fused_computation.clone | custom fusion | bytes 622592 | tf_op jit(solution)/shard_map/jit(_take)/gather | solution.py:116
  552.0 2.8 copy.39
  556.4 9.1 %all-to-all-start.2 = ((f32[3,16,512]{2,0,1:T(4,128)}), f32[3,16,512]{2,0,1:T(4,128)S(1)}, u32[]{:S(2)}, u32[]{:S(2)}) async-start(f32[3,16,512]{2,0,1:T(4,128)} %add_multiply_fusion), calls=%async_computation.2 | async-start | bytes 262144 | tf_op jit(solution)/shard_map/all_to_all | solution.py:123
  565.5 3.4 copy.42
  569.0 44.4 %scatter_custom_fusion = f32[3,1024]{0,1:T(8,128)S(1)} fusion(s32[8192]{0:T(1024)S(1)} %bitcast.120, f32[8192,3]{1,0:T(8,128)} %copy.42, f32[]{:T(128)} %constant.84.clone.1), kind=kCustom, calls=%fused_computation.54 | custom fusion | flops 24576 | bytes 12800 | tf_op jit(solution)/shard_map/scatter-add | solution.py:90
  613.4 2.6 copy.43
  616.0 44.4 %scatter_custom_fusion.1 = f32[3,1024]{0,1:T(8,128)S(1)} fusion(s32[8192]{0:T(1024)S(1)} %bitcast.121, f32[8192,3]{1,0:T(8,128)} %copy.43, f32[]{:T(128)} %constant.84.clone.1), kind=kCustom, calls=%fused_computation.52 | custom fusion | flops 24576 | bytes 12800 | tf_op jit(solution)/shard_map/scatter-add | solution.py:90
  (3709 shorter events, 392.6 us)
Async XLA Ops:
  2.0 481.2 %all-to-all-start = ((s32[16,1,512]{2,1,0:T(1,128)}), s32[16,1,512]{2,1,0:T(1,128)S(1)}, u32[]{:S(2)}, u32[]{:S(2)}) async-start(s32[16,1,512]{2,1,0:T(1,128)} %all_to_all.14), calls=%async_computation | async-start | bytes 65536 | tf_op jit(solution)/shard_map/all_to_all | solution.py:117
  54.0 204.9 %copy-start.1 = (f32[3,1024]{1,0:T(4,128)S(1)}, f32[3,1024]{1,0:T(4,128)}, u32[]{:S(2)}) copy-start(f32[3,1024]{1,0:T(4,128)} %param.19) | copy-start | bytes 36868
  54.0 204.9 %copy-start.3 = (f32[1024]{0:T(1024)S(1)}, f32[1024]{0:T(1024)}, u32[]{:S(2)}) copy-start(f32[1024]{0:T(1024)} %param.20) | copy-start | bytes 12292
  277.2 205.0 %copy-start.4 = (f32[3,1024]{1,0:T(4,128)S(1)}, f32[3,1024]{1,0:T(4,128)}, u32[]{:S(2)}) copy-start(f32[3,1024]{1,0:T(4,128)} %param.18) | copy-start | bytes 36868
  482.1 31.7 %copy-start.2 = (f32[3,1024]{1,0:T(4,128)}, f32[3,1024]{1,0:T(4,128)S(1)}, u32[]{:S(2)}) copy-start(f32[3,1024]{1,0:T(4,128)S(1)} %fusion.25) | copy-start | bytes 36868
  483.3 40.9 %copy-start.5 = (s32[1,1,16]{2,1,0:T(1,128)S(1)}, s32[1,1,16]{2,1,0:T(1,128)}, u32[]{:S(2)}) copy-start(s32[1,1,16]{2,1,0:T(1,128)} %param.23) | copy-start | bytes 196
  514.7 40.1 %copy-start = (s32[1,1,16,512]{3,2,1,0:T(8,128)S(1)}, s32[1,1,16,512]{3,2,1,0:T(8,128)}, u32[]{:S(2)}) copy-start(s32[1,1,16,512]{3,2,1,0:T(8,128)} %param.21) | copy-start | bytes 98308
  514.7 40.2 %all-to-all-start.1 = ((f32[9,16,512]{2,0,1:T(8,128)}), f32[9,16,512]{2,0,1:T(8,128)S(1)}, u32[]{:S(2)}, u32[]{:S(2)}) async-start(f32[9,16,512]{2,0,1:T(8,128)} %select_bitcast_fusion), calls=%async_computation.1 | async-start | bytes 1048576 | tf_op jit(solution)/shard_map/all_to_all | solution.py:119
  556.4 57.0 %all-to-all-start.2 = ((f32[3,16,512]{2,0,1:T(4,128)}), f32[3,16,512]{2,0,1:T(4,128)S(1)}, u32[]{:S(2)}, u32[]{:S(2)}) async-start(f32[3,16,512]{2,0,1:T(4,128)} %add_multiply_fusion), calls=%async_computation.2 | async-start | bytes 262144 | tf_op jit(solution)/shard_map/all_to_all | solution.py:123
where the time goes:
time: 663 us; the launch traced here: 661 us
  other arithmetic  455 us (69%)
  local copies, waits for them, and re-layouts  93.3 us (14%)
  blocking collectives  56.4 us (9%)
  starting transfers between devices  30.1 us (5%)
  loops' own time  25.3 us (4%)
    reduce_sum x512, other arithmetic, dipole_block(): jnp.sum(radial_coef[None] * offset, axis=2)  126 us
    reduce_sum x512, other arithmetic, dipole_block(): radius_sq = jnp.sum(offset * offset, axis=0) + 1.0  97 us
    scatter-add x2, other arithmetic, accumulate(): jnp.zeros((3, particle_count), jnp.float32).at[:, flat_ids].add(flat_values)  88.9 us
    reduce_sum x512, other arithmetic, dipole_block(): jnp.sum(direct_coef[None] * source_mom[:, None, :], axis=2)  76.8 us
    select_n x512, other arithmetic, dipole_block(): direct_coef = jnp.where(keep_mask, inverse_cube, 0.0)  54.2 us
    all_gather x2, blocking collectives, on_device(): lax.all_gather(moments, 'row', axis=1, tiled=True)  35.3 us
    gather x2, local copies, waits for them, and re-layouts, on_device(): looked_up = jnp.take(state_rows, asked_ids, axis=1)  30.5 us
    gather x2, local copies, waits for them, and re-layouts, on_device(): owner_rows = jnp.take(state_rows, owner_ids, axis=1)  30.5 us
  transfers between devices with their start and end apart: 3, of which 0 were waited for; matrix products, arithmetic and copies ran while one was open for 71% of the time, Pallas kernels for 0%

commit v1 on v0

v1 whole, which is shorter than its diff:
```python
import functools

import jax
import jax.numpy as jnp
from jax import lax
from jax.experimental import pallas as pl
from jax.experimental.pallas import tpu as pltpu
from jax.sharding import PartitionSpec as P

F32 = jnp.float32
BF16 = jnp.bfloat16
MESH = pl.DeviceIdType.MESH
CENTRE = 8.0
SRC_BLOCK = 512
TGT_BLOCK = 256


def vmem_specs(count):
    return [pl.BlockSpec(memory_space=pltpu.VMEM)] * count


def peers(axis):
    size = lax.axis_size(axis)
    me = lax.axis_index(axis)
    return [
        (step, lax.rem(me + step, size), lax.rem(me + size - step, size))
        for step in range(1, size)
    ], me


def enter(axes):
    barrier = pltpu.get_barrier_semaphore()
    total = 0
    for axis in axes:
        others, unused = peers(axis)
        for step, target, source in others:
            pl.semaphore_signal(barrier, inc=1, device_id={axis: target}, device_id_type=MESH)
        total += len(others)
    pl.semaphore_wait(barrier, total)


def exchange(axis, source_of, out_ref, send_sem, recv_sem):
    others, me = peers(axis)
    copies = []
    for step, target, source in others:
        copy = pltpu.make_async_remote_copy(
            src_ref=source_of(target),
            dst_ref=out_ref.at[me],
            send_sem=send_sem.at[step],
            recv_sem=recv_sem.at[step],
            device_id={axis: target},
            device_id_type=MESH,
        )
        copy.start()
        copies.append(copy)
    own = pltpu.make_async_copy(source_of(me), out_ref.at[me], send_sem.at[0])
    own.start()
    return copies + [own]


def first_exchange(row_ref, col_ref, list_ref, row_out, col_out, list_out, send_sem, recv_sem):
    enter(("row", "col"))
    copies = exchange("row", lambda t: row_ref, row_out, send_sem.at[0], recv_sem.at[0])
    copies += exchange("col", lambda t: list_ref.at[t], list_out, send_sem.at[1], recv_sem.at[1])
    copies += exchange("col", lambda t: col_ref, col_out, send_sem.at[2], recv_sem.at[2])
    for copy in copies:
        copy.wait()


def one_exchange(axis, block_ref, out_ref, send_sem, recv_sem):
    enter((axis,))
    for copy in exchange(axis, lambda t: block_ref, out_ref, send_sem, recv_sem):
        copy.wait()


def gather_blocks(block, axis, collective_id, size):
    return pl.pallas_call(
        functools.partial(one_exchange, axis),
        out_shape=jax.ShapeDtypeStruct((size,) + block.shape, block.dtype),
        in_specs=vmem_specs(1),
        out_specs=pl.BlockSpec(memory_space=pltpu.VMEM),
        scratch_shapes=[pltpu.SemaphoreType.DMA((size,)), pltpu.SemaphoreType.DMA((size,))],
        compiler_params=pltpu.CompilerParams(collective_id=collective_id, has_side_effects=True),
        name="gather_" + axis + str(collective_id),
    )(block)


def pieces(value, count):
    out = []
    for unused in range(count):
        head = value.astype(BF16)
        wide = head.astype(F32)
        out.append(wide)
        value = value - wide
    return out


def target_rows(pos):
    first, second, third = pieces(-2.0 * pos, 3)
    norm = jnp.sum(pos * pos, axis=0, keepdims=True) + 1.0
    one = jnp.ones_like(norm)
    rows = [first, second, third, first, second, first, one, one, one] + pieces(norm, 3)
    return jnp.concatenate(rows, axis=0).astype(BF16)


def source_rows(pos):
    first, second, third = pieces(pos, 3)
    norm = jnp.sum(pos * pos, axis=0, keepdims=True)
    one = jnp.ones_like(norm)
    rows = [first, first, first, second, second, third] + pieces(norm, 3) + [one, one, one]
    return jnp.concatenate(rows, axis=0).astype(BF16)


def source_weights(pos, mom):
    norm = jnp.sum(pos * pos, axis=0, keepdims=True)
    along = jnp.sum(pos * mom, axis=0, keepdims=True)
    terms = jnp.concatenate(
        [mom, pos[0:1] * mom, pos[1:2] * mom, pos[2:3] * mom, norm * mom, along * pos], axis=0
    )
    return jnp.concatenate(pieces(terms, 3), axis=0).astype(BF16)


def combine(acc, pos):
    sums = acc[0:18] + (acc[18:36] + acc[36:54])
    x, y, z = pos[0:1], pos[1:2], pos[2:3]
    mom = sums[0:3]
    by_x, by_y, by_z = sums[3:6], sums[6:9], sums[9:12]
    norm_mom, along_pos = sums[12:15], sums[15:18]
    inner = x * mom[0:1] + y * mom[1:2] + z * mom[2:3]
    trace = by_x[0:1] + by_y[1:2] + by_z[2:3]
    crossed = jnp.concatenate(
        [x * by[0:1] + y * by[1:2] + z * by[2:3] for by in (by_x, by_y, by_z)], axis=0
    )
    radial = pos * (inner - trace) - crossed + along_pos
    norm = jnp.sum(pos * pos, axis=0, keepdims=True) + 1.0
    direct = norm * mom + norm_mom - 2.0 * (x * by_x + y * by_y + z * by_z)
    return 3.0 * radial - direct


def field_kernel(passes, own_ref, pos_ref, mom_ref, field_ref, rows_ref, weights_ref, target_ref, acc_ref):
    parts, unused, part_len = pos_ref.shape
    mom_at = 3 if pos_ref.shape == mom_ref.shape else 0

    @pl.loop(0, parts)
    def _(part):
        at = pl.ds(pl.multiple_of(part * part_len, part_len), part_len)
        pos = pos_ref[part, 0:3, :]
        mom = mom_ref[part, mom_at : mom_at + 3, :]
        rows_ref[:, at] = source_rows(pos)
        weights_ref[:, at] = source_weights(pos, mom)

    own_pos = own_ref[0:3, :]
    target_ref[...] = target_rows(own_pos)
    acc_ref[...] = jnp.zeros_like(acc_ref)

    @pl.loop(0, parts * part_len // SRC_BLOCK)
    def _(block):
        at = pl.ds(pl.multiple_of(block * SRC_BLOCK, SRC_BLOCK), SRC_BLOCK)
        rows = rows_ref[:, at]
        weights = weights_ref[:, at]
        for start in range(0, part_len, TGT_BLOCK):
            to = slice(start, start + TGT_BLOCK)
            radius_sq = lax.dot_general(
                rows, target_ref[:, to], (((0,), (0,)), ((), ())), preferred_element_type=F32
            )
            inverse = lax.rsqrt(radius_sq)
            square = inverse * inverse
            fifth = square * square * inverse
            head = fifth.astype(BF16)
            added = jnp.dot(weights, head, preferred_element_type=F32)
            if passes == 2:
                tail = (fifth - head.astype(F32)).astype(BF16)
                added = added + jnp.dot(weights, tail, preferred_element_type=F32)
            acc_ref[:, to] += added

    field_ref[0:3, :] = combine(acc_ref[...], own_pos)


def field_of(passes, own, pos_all, mom_all):
    parts, unused, part_len = pos_all.shape
    total = parts * part_len
    return pl.pallas_call(
        functools.partial(field_kernel, passes),
        out_shape=jax.ShapeDtypeStruct((3, part_len), F32),
        in_specs=vmem_specs(3),
        out_specs=pl.BlockSpec(memory_space=pltpu.VMEM),
        scratch_shapes=[
            pltpu.VMEM((24, total), BF16),
            pltpu.VMEM((54, total), BF16),
            pltpu.VMEM((24, part_len), BF16),
            pltpu.VMEM((54, part_len), F32),
        ],
        name="field" + str(passes),
    )(own, pos_all, mom_all)


def picked(table, high, low):
    out = None
    for group, row in enumerate(table):
        found = jnp.take_along_axis(row, low, axis=1)
        out = found if out is None else jnp.where(high == group, found, out)
    return out


def pair_force(mine, other):
    sep = [mine[k] - other[k] for k in range(3)]
    vel = [mine[3 + k] - other[3 + k] for k in range(3)]
    m_one = mine[6:9]
    m_two = other[6:9]

    def dot(a, b):
        return a[0] * b[0] + a[1] * b[1] + a[2] * b[2]

    radius_sq = dot(sep, sep) + 1.0
    inverse = lax.rsqrt(radius_sq)
    distance = radius_sq * inverse
    normal = [s * inverse for s in sep]
    one = dot(m_one, normal)
    two = dot(m_two, normal)
    radial = 3.0 * (dot(m_one, m_two) - 5.0 * one * two)
    radial = radial - 0.03 * (distance - 1.0) - 0.5 * dot(vel, normal)
    return [3.0 * (one * m_two[k] + two * m_one[k]) + radial * normal[k] for k in range(3)]


def contact_kernel(own_ref, mom_ref, col_ref, mom_all_ref, list_ref, back_ref, out_ref, acc_ref):
    columns = col_ref.shape[0]
    half = list_ref.shape[1] // 2
    acc_ref[...] = jnp.zeros_like(acc_ref)

    def table(read):
        return [jnp.broadcast_to(read(slice(g * 128, g * 128 + 128)), (8, 128)) for g in range(8)]

    @pl.loop(0, columns)
    def _(column):
        here = list_ref[column]
        back = back_ref[column]
        my_ids = jnp.concatenate([here[:half], back[half:]], axis=0)
        other_ids = jnp.concatenate([here[half:], back[:half]], axis=0)
        live = my_ids >= 0
        live = jnp.logical_and(live, other_ids >= 0)
        my_high, my_low = my_ids >> 7, my_ids & 127
        other_high, other_low = other_ids >> 7, other_ids & 127
        mine, other = [], []
        for k in range(9):
            if k < 6:
                mine.append(picked(table(lambda s: own_ref[k : k + 1, s]), my_high, my_low))
                other.append(
                    picked(table(lambda s: col_ref[column, k : k + 1, s]), other_high, other_low)
                )
            else:
                j = k - 6
                mine.append(picked(table(lambda s: mom_ref[j : j + 1, s]), my_high, my_low))
                other.append(
                    picked(table(lambda s: mom_all_ref[column, j : j + 1, s]), other_high, other_low)
                )
        force = [jnp.where(live, f, 0.0) for f in pair_force(mine, other)]
        split = [p for f in force for p in pieces(f, 3)]
        group_ids = lax.broadcasted_iota(jnp.int32, (8, 128), 0)
        lane_ids = lax.broadcasted_iota(jnp.int32, (128, 128), 0)
        left, right = [], []
        for k in range(8):
            hit = jnp.broadcast_to(my_high[k : k + 1], (8, 128)) == group_ids
            left.append(
                jnp.concatenate(
                    [jnp.where(hit, jnp.broadcast_to(p[k : k + 1], (8, 128)), 0.0) for p in split], axis=0
                ).astype(BF16)
            )
            same = jnp.broadcast_to(my_low[k : k + 1], (128, 128)) == lane_ids
            right.append(jnp.where(same, 1.0, 0.0).astype(BF16))
        acc_ref[...] += lax.dot_general(
            jnp.concatenate(left, axis=1),
            jnp.concatenate(right, axis=1),
            (((1,), (1,)), ((), ())),
            preferred_element_type=F32,
        )

    for k in range(3):
        base = 24 * k
        total = acc_ref[base : base + 8] + (acc_ref[base + 8 : base + 16] + acc_ref[base + 16 : base + 24])
        for g in range(8):
            out_ref[k : k + 1, g * 128 : g * 128 + 128] = total[g : g + 1]


def contact_forces(own, mom, col_all, mom_all, lists, back):
    return pl.pallas_call(
        contact_kernel,
        out_shape=jax.ShapeDtypeStruct((3, own.shape[1]), F32),
        in_specs=vmem_specs(6),
        out_specs=pl.BlockSpec(memory_space=pltpu.VMEM),
        scratch_shapes=[pltpu.VMEM((72, 128), F32)],
        name="contacts",
    )(own, mom, col_all, mom_all, lists, back)


def on_device(positions, velocity, applied, suscept, contact_owner, contact_partner, contact_count):
    rows = lax.axis_size("row")
    cols = lax.axis_size("col")
    length = positions.shape[1]
    slots = contact_owner.shape[3]
    start = suscept[None, :] * applied
    centred = positions - CENTRE
    row_block = jnp.concatenate([centred, start], axis=0)
    col_block = jnp.concatenate([centred, velocity], axis=0)
    live = jnp.arange(slots, dtype=jnp.int32)[None, :] < contact_count.reshape(cols, 1)
    owners = jnp.where(live, contact_owner.reshape(cols, slots), -1).reshape(cols, slots // 128, 128)
    partners = jnp.where(live, contact_partner.reshape(cols, slots), -1).reshape(cols, slots // 128, 128)
    lists = jnp.concatenate([owners, partners], axis=1)

    row_all, col_all, back = pl.pallas_call(
        first_exchange,
        out_shape=(
            jax.ShapeDtypeStruct((rows, 6, length), F32),
            jax.ShapeDtypeStruct((cols, 6, length), F32),
            jax.ShapeDtypeStruct(lists.shape, jnp.int32),
        ),
        in_specs=vmem_specs(3),
        out_specs=tuple(vmem_specs(3)),
        scratch_shapes=[
            pltpu.SemaphoreType.DMA((3, max(rows, cols))),
            pltpu.SemaphoreType.DMA((3, max(rows, cols))),
        ],
        compiler_params=pltpu.CompilerParams(collective_id=0, has_side_effects=True),
        name="first_exchange",
    )(row_block, col_block, lists)

    field = field_of(2, row_block, row_all, row_all)
    moments = suscept[None, :] * (applied + (field + start))
    mom_row = gather_blocks(moments, "row", 1, rows)
    field = field_of(2, row_block, row_all, mom_row)
    moments = suscept[None, :] * (applied + (field + moments))
    mom_col = gather_blocks(moments, "col", 2, cols)
    forces = contact_forces(col_block, moments, col_all, mom_col, lists, back)
    return (moments, forces)


def solution(mesh):
    placed = (
        P(None, ("col", "row")),
        P(None, ("col", "row")),
        P(None, ("col", "row")),
        P(("col", "row")),
        P("col", "row", None, None),
        P("col", "row", None, None),
        P("col", "row", None),
    )
    return jax.shard_map(
        on_device,
        mesh=mesh,
        in_specs=placed,
        out_specs=(P(None, ("col", "row")), P(None, ("col", "row"))),
        check_vma=False,
    )
```

time: 663 us -> 146 us (0.22)
  other arithmetic: 455 us -> 4.05 us
  Pallas kernels: 0 us -> 138 us
  local copies, waits for them, and re-layouts: 93.3 us -> 2.22 us
  blocking collectives: 56.4 us -> 0 us
  starting transfers between devices: 30.1 us -> 0 us
  loops' own time: 25.3 us -> 0 us
    reduce_sum x1538 -> x0, other arithmetic: 301 us -> none  [the longest x512 126 us: dipole_block(): jnp.sum(radial_coef[None] * offset, axis=2)]
    pallas_call x0 -> x6, Pallas kernels: none -> 138 us  [the longest x2 71.1 us: field_of(): pl.pallas_call(functools.partial(field_kernel, passes), out_shape=jax.Sha...]
    scatter-add x2 -> x0, other arithmetic: 88.9 us -> none  [accumulate(): jnp.zeros((3, particle_count), jnp.float32).at[:, flat_ids].add(flat_values)]
    gather x4 -> x0, local copies, waits for them, and re-layouts: 61.1 us -> none  [the longest x2 30.5 us: on_device(): looked_up = jnp.take(state_rows, asked_ids, axis=1)]
    all_gather x3 -> x0, blocking collectives: 56.4 us -> none  [the longest x2 35.3 us: on_device(): lax.all_gather(moments, 'row', axis=1, tiled=True)]
    select_n x516 -> x1, other arithmetic: 55.2 us -> 0.08 us  [on_device(): jnp.where(live, contact_owner.reshape(cols, slots), -1)]
    all_to_all x3 -> x0, starting transfers between devices: 30.1 us -> none  [the longest x1 11.6 us: on_device(): lax.all_to_all(partner_ids, 'col', split_axis=0, concat_axis=0, tiled=True)]
    another operation x18 -> x0, loops' own time: 25.3 us -> none  [the longest x16 24.8 us: per_target(): lax.scan(add_block, jnp.zeros((3, target_block), jnp.float32), source_blo...]
  transfers between devices with their start and end apart: 3 -> 0, of which waited for: 0 -> 0; matrix products, arithmetic and copies ran while one was open for 71% -> 0% of each run, Pallas kernels for 0% -> 0%
where the time goes in v1:
time: 146 us; the launch traced here: 145 us
  Pallas kernels  138 us (95%)
  other arithmetic  4.05 us (3%)
  local copies, waits for them, and re-layouts  2.22 us (2%)
    pallas_call x2, Pallas kernels, field_of(): pl.pallas_call(functools.partial(field_kernel, passes), out_shape=jax.Sha...  71.1 us
    pallas_call x1, Pallas kernels, on_device(): pl.pallas_call(first_exchange, out_shape=(jax.ShapeDtypeStruct((rows, 6,...  31.3 us
    pallas_call x2, Pallas kernels, gather_blocks(): pl.pallas_call(functools.partial(one_exchange, axis), out_shape=jax.Shape...  25.8 us
    pallas_call x1, Pallas kernels, contact_forces(): pl.pallas_call(contact_kernel, out_shape=jax.ShapeDtypeStruct((3, own.sha...  9.73 us

profile of v1, /device:TPU:1, one launch (start us, length us, event | category | flops | bytes accessed | tf_op | source)
XLA Modules:
  0.0 145.0 jit_solution(2818180856041469924)
XLA Ops:
  0.6 0.0 copy-start.3
  0.7 0.8 reshape.39
  1.4 0.0 copy-done.3
  1.4 0.0 copy-start.6
  1.5 0.6 copy-done.6
  2.1 0.1 compare_select_fusion.1
  2.2 0.0 copy-start.1
  2.2 0.0 copy-start.2
  2.2 0.0 copy-start.4
  2.2 0.6 pad_add_fusion.list_ref
  2.9 0.0 copy-done.1
  2.9 0.0 copy-done.2
  2.9 0.0 copy-done.4
  2.9 0.0 copy-start.5
  3.0 0.7 copy-done.5
  3.7 0.6 pad_maximum_fusion
  4.3 31.3 %first_exchange.1 = (f32[16,6,1024]{2,1,0:T(8,128)}, f32[16,6,1024]{2,1,0:T(8,128)}, s32[16,8,128]{2,1,0:T(8,128)}) custom-call(f32[6,1024]{1,0:T(8,128)} %get-tuple-element.9.row_ref.own_ref, f32[6,1024]{1,0:T(8,128)} %get-tuple-element.8.col_ref.own_ref, s32[16,8,128]{2,1,0:T(8,128)} %pad_add_fusion.list_ref), custom_call_target="tpu_custom_call" | custom-call | tf_op jit(solution)/shard_map/first_exchange/pallas_call | solution.py:309
  35.6 35.6 %field2.2 = f32[3,1024]{1,0:T(4,128)} custom-call(f32[6,1024]{1,0:T(8,128)} %get-tuple-element.9.row_ref.own_ref, f32[16,6,1024]{2,1,0:T(8,128)} %get-tuple-element.5.pos_ref.mom_ref, f32[16,6,1024]{2,1,0:T(8,128)} %get-tuple-element.5.pos_ref.mom_ref), custom_call_target="tpu_custom_call" | custom-call | tf_op jit(solution)/shard_map/field2/pallas_call | solution.py:182
  71.2 1.3 add_multiply_fusion.1.block_ref
  72.5 12.2 %gather_row1.1.mom_ref = f32[16,3,1024]{2,1,0:T(4,128)} custom-call(f32[3,1024]{1,0:T(4,128)} %add_multiply_fusion.1.block_ref), custom_call_target="tpu_custom_call" | custom-call | tf_op jit(solution)/shard_map/gather_row1/pallas_call | solution.py:77
  84.7 0.0 copy-start
  84.7 35.5 %field2.3 = f32[3,1024]{1,0:T(4,128)} custom-call(f32[6,1024]{1,0:T(8,128)} %get-tuple-element.9.row_ref.own_ref, f32[16,6,1024]{2,1,0:T(8,128)} %get-tuple-element.5.pos_ref.mom_ref, f32[16,3,1024]{2,1,0:T(4,128)} %gather_row1.1.mom_ref), custom_call_target="tpu_custom_call" | custom-call | tf_op jit(solution)/shard_map/field2/pallas_call | solution.py:182
  120.2 0.0 copy-done
  120.2 1.3 add_multiply_fusion.block_ref.mom_ref
  121.6 13.7 %gather_col2.1.mom_all_ref = f32[16,3,1024]{2,1,0:T(4,128)} custom-call(f32[3,1024]{1,0:T(4,128)} %add_multiply_fusion.block_ref.mom_ref), custom_call_target="tpu_custom_call" | custom-call | tf_op jit(solution)/shard_map/gather_col2/pallas_call | solution.py:77
  135.2 9.7 %contacts.1 = f32[3,1024]{1,0:T(4,128)} custom-call(f32[6,1024]{1,0:T(8,128)} %get-tuple-element.8.col_ref.own_ref, f32[3,1024]{1,0:T(4,128)} %add_multiply_fusion.block_ref.mom_ref, f32[16,6,1024]{2,1,0:T(8,128)} %get-tuple-element.6.col_ref, f32[16,3,1024]{2,1,0:T(4,128)} %gather_col2.1.mom_all_ref, s32[16,8,128]{2,1,0:T(8,128)} %pad_add_fusion.list_ref, ...), custom_call_target="tpu_custom_call" | custom-call | tf_op jit(solution)/shard_map/contacts/pallas_call | solution.py:285
  (3 shorter events, 0.0 us)
Async XLA Ops:
  0.6 0.8 copy-start.3
  1.4 0.7 copy-start.6
  2.2 0.7 copy-start.1
  2.2 0.7 copy-start.2
  2.2 0.7 copy-start.4
  2.9 0.7 copy-start.5
  84.7 35.5 %copy-start = (f32[3,1024]{1,0:T(4,128)S(1)}, f32[3,1024]{1,0:T(4,128)}, u32[]{:S(2)}) copy-start(f32[3,1024]{1,0:T(4,128)} %field2.2) | copy-start | bytes 36868

commit v2 on v1

v2 whole, which is shorter than its diff:
```python
import functools

import jax
import jax.numpy as jnp
from jax import lax
from jax.experimental import pallas as pl
from jax.experimental.pallas import tpu as pltpu
from jax.sharding import PartitionSpec as P

F32 = jnp.float32
BF16 = jnp.bfloat16
MESH = pl.DeviceIdType.MESH
CENTRE = 8.0
SRC_BLOCK = 512
ROW_SHAPE = (2, 4, 2)
TGT_BLOCK = 256


def vmem_specs(count):
    return [pl.BlockSpec(memory_space=pltpu.VMEM)] * count


def row_steps(step):
    depth, height, cores = ROW_SHAPE
    me = lax.axis_index("row")
    core, rest = lax.rem(me, cores), lax.div(me, cores)
    y, z = lax.rem(rest, height), lax.div(rest, height)
    core_by, rest_by = lax.rem(step, cores), lax.div(step, cores)
    turn, z_by = lax.rem(rest_by, height), lax.div(rest_by, height)
    y_by = turn + lax.div(turn, 2) - 2 * lax.div(turn, 3)

    def at(sign):
        new_z = lax.rem(z + depth + sign * z_by, depth)
        new_y = lax.rem(y + height + sign * y_by, height)
        new_core = lax.rem(core + cores + sign * core_by, cores)
        return (new_z * height + new_y) * cores + new_core

    return at(1), at(-1)


def col_steps(step):
    size = lax.axis_size("col")
    me = lax.axis_index("col")
    return lax.rem(me + step, size), lax.rem(me + size - step, size)


def each_step(axis, body):
    lax.fori_loop(1, lax.axis_size(axis), lambda step, carry: (body(step), carry)[1], 0)


def enter():
    barrier = pltpu.get_barrier_semaphore()

    def signal_row(step):
        pl.semaphore_signal(barrier, inc=1, device_id={"row": row_steps(step)[0]}, device_id_type=MESH)

    def signal_col(step):
        pl.semaphore_signal(barrier, inc=1, device_id={"col": col_steps(step)[0]}, device_id_type=MESH)

    each_step("row", signal_row)
    each_step("col", signal_col)
    pl.semaphore_wait(barrier, lax.axis_size("row") + lax.axis_size("col") - 2)


def pieces(value, count):
    out = []
    for unused in range(count):
        head = value.astype(BF16)
        wide = head.astype(F32)
        out.append(wide)
        value = value - wide
    return out


def target_rows(pos):
    first, second, third = pieces(-2.0 * pos, 3)
    norm = jnp.sum(pos * pos, axis=0, keepdims=True) + 1.0
    one = jnp.ones_like(norm)
    rows = [first, second, third, first, second, first, one, one, one] + pieces(norm, 3)
    return jnp.concatenate(rows, axis=0).astype(BF16)


def source_rows(pos):
    first, second, third = pieces(pos, 3)
    norm = jnp.sum(pos * pos, axis=0, keepdims=True)
    one = jnp.ones_like(norm)
    rows = [first, first, first, second, second, third] + pieces(norm, 3) + [one, one, one]
    return jnp.concatenate(rows, axis=0).astype(BF16)


def source_weights(pos, mom):
    norm = jnp.sum(pos * pos, axis=0, keepdims=True)
    along = jnp.sum(pos * mom, axis=0, keepdims=True)
    terms = jnp.concatenate(
        [mom, pos[0:1] * mom, pos[1:2] * mom, pos[2:3] * mom, norm * mom, along * pos], axis=0
    )
    return jnp.concatenate(pieces(terms, 3), axis=0).astype(BF16)


def combine(acc, pos):
    sums = acc[0:18] + (acc[18:36] + acc[36:54])
    x, y, z = pos[0:1], pos[1:2], pos[2:3]
    mom = sums[0:3]
    by_x, by_y, by_z = sums[3:6], sums[6:9], sums[9:12]
    norm_mom, along_pos = sums[12:15], sums[15:18]
    inner = x * mom[0:1] + y * mom[1:2] + z * mom[2:3]
    trace = by_x[0:1] + by_y[1:2] + by_z[2:3]
    crossed = jnp.concatenate(
        [x * by[0:1] + y * by[1:2] + z * by[2:3] for by in (by_x, by_y, by_z)], axis=0
    )
    radial = pos * (inner - trace) - crossed + along_pos
    norm = jnp.sum(pos * pos, axis=0, keepdims=True) + 1.0
    direct = norm * mom + norm_mom - 2.0 * (x * by_x + y * by_y + z * by_z)
    return 3.0 * radial - direct


def add_field(rows_ref, weights_ref, target_ref, acc_ref, first, count, targets):
    sums = {}
    for start in range(0, count, SRC_BLOCK):
        at = pl.ds(pl.multiple_of(first + start, SRC_BLOCK), SRC_BLOCK)
        rows = rows_ref[:, at]
        weights = weights_ref[:, at]
        for low in range(targets[0], targets[1], TGT_BLOCK):
            to = slice(low, low + TGT_BLOCK)
            radius_sq = lax.dot_general(
                rows, target_ref[:, to], (((0,), (0,)), ((), ())), preferred_element_type=F32
            )
            inverse = lax.rsqrt(radius_sq)
            square = inverse * inverse
            fifth = square * square * inverse
            head = fifth.astype(BF16)
            tail = (fifth - head.astype(F32)).astype(BF16)
            acc_ref[:, to] += jnp.dot(weights, head, preferred_element_type=F32) + jnp.dot(
                weights, tail, preferred_element_type=F32
            )


def induce(
    pos_ref, vel_ref, app_ref, sus_ref, own_ref, part_ref,
    mom_ref, pos_cols, vel_cols, mom_cols, own_back, part_back,
    block_ref, block_all, first_ref, first_all, second_ref, rows_ref, weights_ref, target_ref, acc_ref,
    row_send, row_recv, one_send, one_recv, col_send, col_recv, two_send, two_recv, local_sem,
):
    length = pos_ref.shape[1]
    half = length // 2
    parts = block_all.shape[0]
    here = lax.axis_index("row")
    column = lax.axis_index("col")

    pos = pos_ref[...] - CENTRE
    start = sus_ref[...] * app_ref[...]
    block_ref[0:3, :] = pos
    block_ref[3:6, :] = start
    target_ref[...] = target_rows(pos)
    acc_ref[...] = jnp.zeros_like(acc_ref)
    enter()

    def row_copy(source, gathered, send, recv, step):
        to = row_steps(step)[0]
        return pltpu.make_async_remote_copy(
            src_ref=source, dst_ref=gathered.at[here], send_sem=send.at[step], recv_sem=recv.at[step],
            device_id={"row": to}, device_id_type=MESH,
        )

    def row_arrival(source, gathered, send, recv, step):
        to, origin = row_steps(step)
        return pltpu.make_async_remote_copy(
            src_ref=source, dst_ref=gathered.at[origin], send_sem=send.at[step], recv_sem=recv.at[step],
            device_id={"row": to}, device_id_type=MESH,
        )

    row_args = (block_ref, block_all, row_send, row_recv)
    one_args = (first_ref, first_all, one_send, one_recv)
    each_step("row", lambda step: row_copy(*row_args, step).start())

    def col_pairs(to, origin):
        return (
            (pos_ref, pos_cols.at[:, origin, :]),
            (vel_ref, vel_cols.at[:, origin, :]),
            (own_ref.at[pl.ds(to, 1)], own_back.at[pl.ds(origin, 1)]),
            (part_ref.at[pl.ds(to, 1)], part_back.at[pl.ds(origin, 1)]),
        )

    def col_copies(to, origin, step):
        return [
            pltpu.make_async_remote_copy(
                src_ref=source, dst_ref=target, send_sem=col_send.at[k, step], recv_sem=col_recv.at[k, step],
                device_id={"col": to}, device_id_type=MESH,
            )
            for k, (source, target) in enumerate(col_pairs(to, origin))
        ]

    def col_start(step):
        for copy in col_copies(col_steps(step)[0], column, step):
            copy.start()

    def own_copies():
        return [
            pltpu.make_async_copy(source, target, local_sem.at[k])
            for k, (source, target) in enumerate(col_pairs(column, column))
        ]

    def two_copy(part, to, origin, step):
        return pltpu.make_async_remote_copy(
            src_ref=second_ref.at[part], dst_ref=mom_cols.at[part, :, origin, :],
            send_sem=two_send.at[part, step], recv_sem=two_recv.at[part, step],
            device_id={"col": to}, device_id_type=MESH,
        )

    def two_own(part):
        return pltpu.make_async_copy(second_ref.at[part], mom_cols.at[part, :, column, :], local_sem.at[4 + part])

    def two_start(part):
        each_step("col", lambda step: two_copy(part, col_steps(step)[0], column, step).start())
        two_own(part).start()

    def prepare(step, pos, mom, with_rows):
        at = pl.ds(pl.multiple_of(step * length, length), length)
        if with_rows:
            rows_ref[:, at] = source_rows(pos)
        weights_ref[:, at] = source_weights(pos, mom)

    prepare(0, pos, start, True)

    @pl.loop(0, parts)
    def _(step):
        @pl.when(step > 0)
        def _():
            row_arrival(*row_args, step).wait_recv()
            origin = row_steps(step)[1]
            prepare(step, block_all[origin, 0:3, :], block_all[origin, 3:6, :], True)

        @pl.when(step == 4)
        def _():
            each_step("col", col_start)
            for copy in own_copies():
                copy.start()

        add_field(rows_ref, weights_ref, target_ref, acc_ref, step * length, length, (0, length))

    field = combine(acc_ref[...], pos)
    first = sus_ref[...] * (app_ref[...] + (field + start))
    first_ref[...] = first
    prepare(0, pos, first, False)
    acc_ref[...] = jnp.zeros_like(acc_ref)
    each_step("row", lambda step: row_copy(*one_args, step).start())

    def finish(part):
        at = slice(part * half, part * half + half)
        field = combine(acc_ref[:, at], pos_ref[:, at] - CENTRE)
        second = sus_ref[:, at] * (app_ref[:, at] + (field + first_ref[:, at]))
        second_ref[part] = second
        mom_ref[:, at] = second

    @pl.loop(0, parts)
    def _(step):
        @pl.when(step > 0)
        def _():
            row_arrival(*one_args, step).wait_recv()
            origin = row_steps(step)[1]
            prepare(step, block_all[origin, 0:3, :], first_all[origin], False)

        add_field(rows_ref, weights_ref, target_ref, acc_ref, step * length, length, (0, half))

    finish(0)

    @pl.loop(0, parts // 2)
    def _(step):
        @pl.when(step == 1)
        def _():
            two_start(0)

        add_field(rows_ref, weights_ref, target_ref, acc_ref, step * 2 * length, 2 * length, (half, length))

    finish(1)

    def row_done(step):
        row_copy(*row_args, step).wait_send()
        row_copy(*one_args, step).wait_send()

    each_step("row", row_done)
    two_start(1)

    def col_done(step):
        to, origin = col_steps(step)
        for copy in col_copies(to, origin, step):
            copy.wait()

    each_step("col", col_done)
    for copy in own_copies():
        copy.wait()
    for part in range(2):
        each_step("col", lambda step: two_copy(part, *col_steps(step), step).wait())
        two_own(part).wait()


def picked(table, high, low):
    out = None
    for group, row in enumerate(table):
        found = jnp.take_along_axis(row, low, axis=1)
        out = found if out is None else jnp.where(high == group, found, out)
    return out


def pair_force(mine, other):
    sep = [mine[k] - other[k] for k in range(3)]
    vel = [mine[3 + k] - other[3 + k] for k in range(3)]
    m_one = mine[6:9]
    m_two = other[6:9]

    def dot(a, b):
        return a[0] * b[0] + a[1] * b[1] + a[2] * b[2]

    radius_sq = dot(sep, sep) + 1.0
    inverse = lax.rsqrt(radius_sq)
    distance = radius_sq * inverse
    normal = [s * inverse for s in sep]
    one = dot(m_one, normal)
    two = dot(m_two, normal)
    radial = 3.0 * (dot(m_one, m_two) - 5.0 * one * two)
    radial = radial - 0.03 * (distance - 1.0) - 0.5 * dot(vel, normal)
    return [3.0 * (one * m_two[k] + two * m_one[k]) + radial * normal[k] for k in range(3)]


def contact_kernel(
    pos_ref, vel_ref, mom_ref, pos_cols, vel_cols, mom_cols, own_ref, part_ref, own_back, part_back, out_ref, acc_ref
):
    columns = pos_cols.shape[1]
    length = pos_ref.shape[1]
    half = length // 2
    chunks = own_ref.shape[1] // 128
    acc_ref[...] = jnp.zeros_like(acc_ref)
    group_ids = lax.broadcasted_iota(jnp.int32, (8, 128), 0)
    lane_ids = lax.broadcasted_iota(jnp.int32, (128, 128), 0)
    groups = [slice(g * 128, g * 128 + 128) for g in range(length // 128)]

    def slots(my_ids, other_ids, live, eight):
        my_high, my_low = my_ids >> 7, my_ids & 127
        other_high, other_low = other_ids >> 7, other_ids & 127
        mine, other = [], []
        for k in range(9):
            if k < 6:
                near, far = (pos_ref, pos_cols) if k < 3 else (vel_ref, vel_cols)
                j = k % 3
                theirs = [far[j, eight, g] for g in groups]
            else:
                near, j = mom_ref, k - 6
                theirs = [mom_cols[g.start // half, j, eight, g.start % half : g.start % half + 128] for g in groups]
            ours = [jnp.broadcast_to(near[j : j + 1, g], (8, 128)) for g in groups]
            mine.append(picked(ours, my_high, my_low))
            other.append(picked(theirs, other_high, other_low))
        force = [jnp.where(live, f, 0.0) for f in pair_force(mine, other)]
        split = [p for f in force for p in pieces(f, 3)]
        left, right = [], []
        for k in range(8):
            hit = jnp.broadcast_to(my_high[k : k + 1], (8, 128)) == group_ids
            left.append(
                jnp.concatenate(
                    [jnp.where(hit, jnp.broadcast_to(p[k : k + 1], (8, 128)), 0.0) for p in split], axis=0
                ).astype(BF16)
            )
            same = jnp.broadcast_to(my_low[k : k + 1], (128, 128)) == lane_ids
            right.append(jnp.where(same, 1.0, 0.0).astype(BF16))
        acc_ref[...] += lax.dot_general(
            jnp.concatenate(left, axis=1),
            jnp.concatenate(right, axis=1),
            (((1,), (1,)), ((), ())),
            preferred_element_type=F32,
        )

    @pl.loop(0, columns // 8 * chunks)
    def _(unit):
        eight = pl.ds(pl.multiple_of(lax.div(unit, chunks) * 8, 8), 8)
        at = pl.ds(pl.multiple_of(lax.rem(unit, chunks) * 128, 128), 128)
        owner, partner = own_ref[eight, at], part_ref[eight, at]
        slots(owner, partner, owner >= 0, eight)
        owner, partner = own_back[eight, at], part_back[eight, at]
        slots(partner, owner, owner >= 0, eight)

    for k in range(3):
        base = 24 * k
        total = acc_ref[base : base + 8] + (acc_ref[base + 8 : base + 16] + acc_ref[base + 16 : base + 24])
        for g in range(8):
            out_ref[k : k + 1, g * 128 : g * 128 + 128] = total[g : g + 1]


def on_device(positions, velocity, applied, suscept, contact_owner, contact_partner, contact_count):
    rows = lax.axis_size("row")
    cols = lax.axis_size("col")
    length = positions.shape[1]
    slots = contact_owner.shape[3]
    live = jnp.arange(slots, dtype=jnp.int32)[None, :] < contact_count.reshape(cols, 1)
    owners = jnp.where(live, contact_owner.reshape(cols, slots), -1)
    partners = contact_partner.reshape(cols, slots)
    copies = pltpu.SemaphoreType.DMA
    vector = jax.ShapeDtypeStruct((3, length), F32)
    per_column = jax.ShapeDtypeStruct((3, cols, length), F32)
    moments, pos_cols, vel_cols, mom_cols, own_back, part_back = pl.pallas_call(
        induce,
        out_shape=(
            vector,
            per_column,
            per_column,
            jax.ShapeDtypeStruct((2, 3, cols, length // 2), F32),
            jax.ShapeDtypeStruct((cols, slots), jnp.int32),
            jax.ShapeDtypeStruct((cols, slots), jnp.int32),
        ),
        in_specs=vmem_specs(6),
        out_specs=tuple(vmem_specs(6)),
        scratch_shapes=[
            pltpu.VMEM((6, length), F32),
            pltpu.VMEM((rows, 6, length), F32),
            pltpu.VMEM((3, length), F32),
            pltpu.VMEM((rows, 3, length), F32),
            pltpu.VMEM((2, 3, length // 2), F32),
            pltpu.VMEM((24, rows * length), BF16),
            pltpu.VMEM((54, rows * length), BF16),
            pltpu.VMEM((24, length), BF16),
            pltpu.VMEM((54, length), F32),
            copies((rows,)), copies((rows,)), copies((rows,)), copies((rows,)),
            copies((4, cols)), copies((4, cols)), copies((2, cols)), copies((2, cols)),
            copies((6,)),
        ],
        compiler_params=pltpu.CompilerParams(collective_id=0, has_side_effects=True),
        name="induce",
    )(positions, velocity, applied, suscept.reshape(1, length), owners, partners)
    forces = pl.pallas_call(
        contact_kernel,
        out_shape=vector,
        in_specs=vmem_specs(10),
        out_specs=pl.BlockSpec(memory_space=pltpu.VMEM),
        scratch_shapes=[pltpu.VMEM((72, 128), F32)],
        name="contacts",
    )(positions, velocity, moments, pos_cols, vel_cols, mom_cols, owners, partners, own_back, part_back)
    return (moments, forces)


def solution(mesh):
    placed = (
        P(None, ("col", "row")),
        P(None, ("col", "row")),
        P(None, ("col", "row")),
        P(("col", "row")),
        P("col", "row", None, None),
        P("col", "row", None, None),
        P("col", "row", None),
    )
    return jax.shard_map(
        on_device,
        mesh=mesh,
        in_specs=placed,
        out_specs=(P(None, ("col", "row")), P(None, ("col", "row"))),
        check_vma=False,
    )
```

time: 146 us -> 93 us (0.64)
  Pallas kernels: 138 us -> 89.4 us
  other arithmetic: 4.05 us -> 1.44 us
    pallas_call x6 -> x2, Pallas kernels: 138 us -> 89.4 us  [the longest x1 81.4 us: on_device(): pl.pallas_call(induce, out_shape=(vector, per_column, per_column, jax.Sha...]
    mul x2 -> x0, other arithmetic: 2.67 us -> none  [the longest x1 1.34 us: on_device(): moments = suscept[None, :] * (applied + (field + moments))]
where the time goes in v2:
time: 93 us; the launch traced here: 92.8 us
  Pallas kernels  89.4 us (96%)
  other arithmetic  1.44 us (2%)
  local copies, waits for them, and re-layouts  1.26 us (1%)
    pallas_call x1, Pallas kernels, on_device(): pl.pallas_call(induce, out_shape=(vector, per_column, per_column, jax.Sha...  81.4 us
    pallas_call x1, Pallas kernels, on_device(): pl.pallas_call(contact_kernel, out_shape=vector, in_specs=vmem_specs(10),...  8.01 us

profile of v2, /device:TPU:1, one launch (start us, length us, event | category | flops | bytes accessed | tf_op | source)
XLA Modules:
  0.0 92.8 jit_solution(8054863504012455436)
XLA Ops:
  0.6 0.0 copy-start.1
  0.6 0.6 copy-done.1
  1.3 1.4 %bitcast_select_fusion.own_ref = s32[16,512]{1,0:T(8,128)} fusion(s32[1,1,16,512]{3,2,1,0:T(8,128)} %param.11, s32[16]{0:T(128)S(1)} %bitcast.8), kind=kLoop, calls=%fused_computation | loop fusion | flops 16384 | bytes 65600 | tf_op jit(solution)/shard_map/jit(_where)/select_n | solution.py:393
  2.7 81.4 %induce.1 = (f32[3,1024]{1,0:T(4,128)}, f32[3,16,1024]{2,1,0:T(8,128)}, f32[3,16,1024]{2,1,0:T(8,128)}, f32[2,3,16,512]{3,2,1,0:T(8,128)}, s32[16,512]{1,0:T(8,128)}, /*index=5*/s32[16,512]{1,0:T(8,128)}) custom-call(f32[3,1024]{1,0:T(4,128)} %pos_ref.3, f32[3,1024]{1,0:T(4,128)} %vel_ref.3, f32[3,1024]{1,0:T(4,128)} %app_ref.1, f32[1,1024]{1,0:T(1,128)} %bitcast.7, ...), custom_call_target="tpu_custom_call" | custom-call | tf_op jit(solution)/shard_map/induce/pallas_call | solution.py:398
  84.1 0.0 copy-start
  84.2 8.0 %contacts.1 = f32[3,1024]{1,0:T(4,128)} custom-call(f32[3,1024]{1,0:T(4,128)} %pos_ref.3, f32[3,1024]{1,0:T(4,128)} %vel_ref.3, f32[3,1024]{1,0:T(4,128)} %get-tuple-element.16.mom_ref, f32[3,16,1024]{2,1,0:T(8,128)} %get-tuple-element.9.pos_cols, f32[3,16,1024]{2,1,0:T(8,128)} %get-tuple-element.10.vel_cols, f32[2,3,16,512]{3,2,1,0:T(8,128)} %get-tuple-element.11.mom_cols, ...), custom_call_target="tpu_custom_call" | custom-call | tf_op jit(solution)/shard_map/contacts/pallas_call | solution.py:427
  92.2 0.0 copy-done
  92.2 0.6 copy.10
Async XLA Ops:
  0.6 0.7 copy-start.1
  84.1 8.0 %copy-start = (f32[3,1024]{1,0:T(4,128)S(1)}, f32[3,1024]{1,0:T(4,128)}, u32[]{:S(2)}) copy-start(f32[3,1024]{1,0:T(4,128)} %get-tuple-element.16.mom_ref) | copy-start | bytes 36868

commit v3 on v2

--- a/solution.py
+++ b/solution.py
@@ -13,6 +13,7 @@
 CENTRE = 8.0
 SRC_BLOCK = 512
 ROW_SHAPE = (2, 4, 2)
+KEPT = 14
 TGT_BLOCK = 256
 
 
@@ -59,7 +60,6 @@
 
     each_step("row", signal_row)
     each_step("col", signal_col)
-    pl.semaphore_wait(barrier, lax.axis_size("row") + lax.axis_size("col") - 2)
 
 
 def pieces(value, count):
@@ -92,30 +92,35 @@
     norm = jnp.sum(pos * pos, axis=0, keepdims=True)
     along = jnp.sum(pos * mom, axis=0, keepdims=True)
     terms = jnp.concatenate(
-        [mom, pos[0:1] * mom, pos[1:2] * mom, pos[2:3] * mom, norm * mom, along * pos], axis=0
+        [mom, pos[0:1] * mom, pos[1:2] * mom, pos[2:3] * mom, 3.0 * (along * pos) - norm * mom], axis=0
     )
     return jnp.concatenate(pieces(terms, 3), axis=0).astype(BF16)
 
 
 def combine(acc, pos):
-    sums = acc[0:18] + (acc[18:36] + acc[36:54])
+    sums = acc[0:15] + (acc[15:30] + acc[30:45])
     x, y, z = pos[0:1], pos[1:2], pos[2:3]
     mom = sums[0:3]
     by_x, by_y, by_z = sums[3:6], sums[6:9], sums[9:12]
-    norm_mom, along_pos = sums[12:15], sums[15:18]
+    mixed = sums[12:15]
     inner = x * mom[0:1] + y * mom[1:2] + z * mom[2:3]
     trace = by_x[0:1] + by_y[1:2] + by_z[2:3]
     crossed = jnp.concatenate(
         [x * by[0:1] + y * by[1:2] + z * by[2:3] for by in (by_x, by_y, by_z)], axis=0
     )
-    radial = pos * (inner - trace) - crossed + along_pos
+    radial = pos * (inner - trace) - crossed
     norm = jnp.sum(pos * pos, axis=0, keepdims=True) + 1.0
-    direct = norm * mom + norm_mom - 2.0 * (x * by_x + y * by_y + z * by_z)
-    return 3.0 * radial - direct
-
-
-def add_field(rows_ref, weights_ref, target_ref, acc_ref, first, count, targets):
-    sums = {}
+    direct = norm * mom - 2.0 * (x * by_x + y * by_y + z * by_z)
+    return 3.0 * radial - direct + mixed
+
+
+def add_sums(weights, head, tail, acc_ref, to):
+    acc_ref[:, to] += jnp.dot(weights, head, preferred_element_type=F32) + jnp.dot(
+        weights, tail, preferred_element_type=F32
+    )
+
+
+def add_field(rows_ref, weights_ref, target_ref, acc_ref, first, count, targets, kept=None):
     for start in range(0, count, SRC_BLOCK):
         at = pl.ds(pl.multiple_of(first + start, SRC_BLOCK), SRC_BLOCK)
         rows = rows_ref[:, at]
@@ -130,15 +135,24 @@
             fifth = square * square * inverse
             head = fifth.astype(BF16)
             tail = (fifth - head.astype(F32)).astype(BF16)
-            acc_ref[:, to] += jnp.dot(weights, head, preferred_element_type=F32) + jnp.dot(
-                weights, tail, preferred_element_type=F32
-            )
+            if kept is not None:
+                kept[0][at, to] = head
+                kept[1][at, to] = tail
+            add_sums(weights, head, tail, acc_ref, to)
+
+
+def add_kept(kept, weights_ref, acc_ref, first, count, targets):
+    at = pl.ds(pl.multiple_of(first, count), count)
+    weights = weights_ref[:, at]
+    for low in range(targets[0], targets[1], TGT_BLOCK):
+        to = slice(low, low + TGT_BLOCK)
+        add_sums(weights, kept[0][at, to], kept[1][at, to], acc_ref, to)
 
 
 def induce(
     pos_ref, vel_ref, app_ref, sus_ref, own_ref, part_ref,
     mom_ref, pos_cols, vel_cols, mom_cols, own_back, part_back,
-    block_ref, block_all, first_ref, first_all, second_ref, rows_ref, weights_ref, target_ref, acc_ref,
+    block_ref, block_all, first_ref, first_all, second_ref, rows_ref, weights_ref, target_ref, acc_ref, heads, tails,
     row_send, row_recv, one_send, one_recv, col_send, col_recv, two_send, two_recv, local_sem,
 ):
     length = pos_ref.shape[1]
@@ -147,13 +161,14 @@
     here = lax.axis_index("row")
     column = lax.axis_index("col")
 
+    enter()
     pos = pos_ref[...] - CENTRE
     start = sus_ref[...] * app_ref[...]
     block_ref[0:3, :] = pos
     block_ref[3:6, :] = start
     target_ref[...] = target_rows(pos)
     acc_ref[...] = jnp.zeros_like(acc_ref)
-    enter()
+    kept = (heads, tails)
 
     def row_copy(source, gathered, send, recv, step):
         to = row_steps(step)[0]
@@ -171,8 +186,6 @@
 
     row_args = (block_ref, block_all, row_send, row_recv)
     one_args = (first_ref, first_all, one_send, one_recv)
-    each_step("row", lambda step: row_copy(*row_args, step).start())
-
     def col_pairs(to, origin):
         return (
             (pos_ref, pos_cols.at[:, origin, :]),
@@ -221,14 +234,19 @@
         weights_ref[:, at] = source_weights(pos, mom)
 
     prepare(0, pos, start, True)
-
-    @pl.loop(0, parts)
+    pl.semaphore_wait(pltpu.get_barrier_semaphore(), lax.axis_size("row") + lax.axis_size("col") - 2)
+    each_step("row", lambda step: row_copy(*row_args, step).start())
+
+    def take_first(step):
+        row_arrival(*row_args, step).wait_recv()
+        origin = row_steps(step)[1]
+        prepare(step, block_all[origin, 0:3, :], block_all[origin, 3:6, :], True)
+
+    @pl.loop(0, KEPT)
     def _(step):
         @pl.when(step > 0)
         def _():
-            row_arrival(*row_args, step).wait_recv()
-            origin = row_steps(step)[1]
-            prepare(step, block_all[origin, 0:3, :], block_all[origin, 3:6, :], True)
+            take_first(step)
 
         @pl.when(step == 4)
         def _():
@@ -236,6 +254,11 @@
             for copy in own_copies():
                 copy.start()
 
+        add_field(rows_ref, weights_ref, target_ref, acc_ref, step * length, length, (0, length), kept)
+
+    @pl.loop(KEPT, parts)
+    def _(step):
+        take_first(step)
         add_field(rows_ref, weights_ref, target_ref, acc_ref, step * length, length, (0, length))
 
     field = combine(acc_ref[...], pos)
@@ -252,26 +275,35 @@
         second_ref[part] = second
         mom_ref[:, at] = second
 
-    @pl.loop(0, parts)
+    def take_second(step):
+        row_arrival(*one_args, step).wait_recv()
+        origin = row_steps(step)[1]
+        prepare(step, block_all[origin, 0:3, :], first_all[origin], False)
+
+    @pl.loop(0, KEPT)
     def _(step):
         @pl.when(step > 0)
         def _():
-            row_arrival(*one_args, step).wait_recv()
-            origin = row_steps(step)[1]
-            prepare(step, block_all[origin, 0:3, :], first_all[origin], False)
-
+            take_second(step)
+
+        add_kept(kept, weights_ref, acc_ref, step * length, length, (0, half))
+
+    @pl.loop(KEPT, parts)
+    def _(step):
+        take_second(step)
         add_field(rows_ref, weights_ref, target_ref, acc_ref, step * length, length, (0, half))
 
     finish(0)
 
-    @pl.loop(0, parts // 2)
+    @pl.loop(0, KEPT // 2)
     def _(step):
         @pl.when(step == 1)
         def _():
             two_start(0)
 
-        add_field(rows_ref, weights_ref, target_ref, acc_ref, step * 2 * length, 2 * length, (half, length))
-
+        add_kept(kept, weights_ref, acc_ref, step * 2 * length, 2 * length, (half, length))
+
+    add_field(rows_ref, weights_ref, target_ref, acc_ref, KEPT * length, (parts - KEPT) * length, (half, length))
     finish(1)
 
     def row_done(step):
@@ -414,14 +446,18 @@
             pltpu.VMEM((rows, 3, length), F32),
             pltpu.VMEM((2, 3, length // 2), F32),
             pltpu.VMEM((24, rows * length), BF16),
-            pltpu.VMEM((54, rows * length), BF16),
+            pltpu.VMEM((45, rows * length), BF16),
             pltpu.VMEM((24, length), BF16),
-            pltpu.VMEM((54, length), F32),
+            pltpu.VMEM((45, length), F32),
+            pltpu.VMEM((KEPT * length, length), BF16),
+            pltpu.VMEM((KEPT * length, length), BF16),
             copies((rows,)), copies((rows,)), copies((rows,)), copies((rows,)),
             copies((4, cols)), copies((4, cols)), copies((2, cols)), copies((2, cols)),
             copies((6,)),
         ],
-        compiler_params=pltpu.CompilerParams(collective_id=0, has_side_effects=True),
+        compiler_params=pltpu.CompilerParams(
+            collective_id=0, has_side_effects=True, vmem_limit_bytes=67043328
+        ),
         name="induce",
     )(positions, velocity, applied, suscept.reshape(1, length), owners, partners)
     forces = pl.pallas_call(

time: 93 us -> 78.8 us (0.85)
  Pallas kernels: 89.4 us -> 75.2 us
    pallas_call x1, Pallas kernels: 81.4 us -> 67.2 us  [on_device(): pl.pallas_call(induce, out_shape=(vector, per_column, per_column, jax.Sha...]
where the time goes in v3:
time: 78.8 us; the launch traced here: 78.5 us
  Pallas kernels  75.2 us (95%)
  other arithmetic  1.44 us (2%)
  local copies, waits for them, and re-layouts  1.26 us (2%)
    pallas_call x1, Pallas kernels, on_device(): pl.pallas_call(induce, out_shape=(vector, per_column, per_column, jax.Sha...  67.2 us
    pallas_call x1, Pallas kernels, on_device(): pl.pallas_call(contact_kernel, out_shape=vector, in_specs=vmem_specs(10),...  8 us

profile of v3, /device:TPU:1, one launch (start us, length us, event | category | flops | bytes accessed | tf_op | source)
XLA Modules:
  0.0 78.5 jit_solution(2515065157164659750)
XLA Ops:
  0.6 0.0 copy-start.1
  0.6 0.6 copy-done.1
  1.3 1.4 %bitcast_select_fusion.own_ref = s32[16,512]{1,0:T(8,128)} fusion(s32[1,1,16,512]{3,2,1,0:T(8,128)} %param.11, s32[16]{0:T(128)S(1)} %bitcast.8), kind=kLoop, calls=%fused_computation | loop fusion | flops 16384 | bytes 65600 | tf_op jit(solution)/shard_map/jit(_where)/select_n | solution.py:425
  2.7 67.2 %induce.1 = (f32[3,1024]{1,0:T(4,128)}, f32[3,16,1024]{2,1,0:T(8,128)}, f32[3,16,1024]{2,1,0:T(8,128)}, f32[2,3,16,512]{3,2,1,0:T(8,128)}, s32[16,512]{1,0:T(8,128)}, /*index=5*/s32[16,512]{1,0:T(8,128)}) custom-call(f32[3,1024]{1,0:T(4,128)} %pos_ref.3, f32[3,1024]{1,0:T(4,128)} %vel_ref.3, f32[3,1024]{1,0:T(4,128)} %app_ref.1, f32[1,1024]{1,0:T(1,128)} %bitcast.7, ...), custom_call_target="tpu_custom_call" | custom-call | tf_op jit(solution)/shard_map/induce/pallas_call | solution.py:430
  69.9 0.0 copy-start
  69.9 8.0 %contacts.1 = f32[3,1024]{1,0:T(4,128)} custom-call(f32[3,1024]{1,0:T(4,128)} %pos_ref.3, f32[3,1024]{1,0:T(4,128)} %vel_ref.3, f32[3,1024]{1,0:T(4,128)} %get-tuple-element.16.mom_ref, f32[3,16,1024]{2,1,0:T(8,128)} %get-tuple-element.9.pos_cols, f32[3,16,1024]{2,1,0:T(8,128)} %get-tuple-element.10.vel_cols, f32[2,3,16,512]{3,2,1,0:T(8,128)} %get-tuple-element.11.mom_cols, ...), custom_call_target="tpu_custom_call" | custom-call | tf_op jit(solution)/shard_map/contacts/pallas_call | solution.py:463
  77.9 0.0 copy-done
  77.9 0.6 copy.10
Async XLA Ops:
  0.6 0.7 copy-start.1
  69.9 8.0 %copy-start = (f32[3,1024]{1,0:T(4,128)S(1)}, f32[3,1024]{1,0:T(4,128)}, u32[]{:S(2)}) copy-start(f32[3,1024]{1,0:T(4,128)} %get-tuple-element.16.mom_ref) | copy-start | bytes 36868

commit v4 on v3

--- a/solution.py
+++ b/solution.py
@@ -149,9 +149,60 @@
         add_sums(weights, kept[0][at, to], kept[1][at, to], acc_ref, to)
 
 
+def picked(table, high, low, first=0):
+    out = None
+    for group, row in enumerate(table):
+        found = jnp.take_along_axis(row, low, axis=1)
+        out = found if out is None else jnp.where(high == first + group, found, out)
+    return out
+
+
+def dot3(a, b):
+    return a[0] * b[0] + a[1] * b[1] + a[2] * b[2]
+
+
+def geometry(mine, other, live):
+    sep = [mine[k] - other[k] for k in range(3)]
+    vel = [mine[3 + k] - other[3 + k] for k in range(3)]
+    radius_sq = dot3(sep, sep) + 1.0
+    inverse = lax.rsqrt(radius_sq)
+    normal = [jnp.where(live, s * inverse, 0.0) for s in sep]
+    return normal + [-0.03 * (radius_sq * inverse - 1.0) - 0.5 * dot3(vel, normal)]
+
+
+def pair_force(normal, along, m_one, m_two):
+    one = dot3(m_one, normal)
+    two = dot3(m_two, normal)
+    radial = 3.0 * (dot3(m_one, m_two) - 5.0 * one * two) + along
+    return [3.0 * (one * m_two[k] + two * m_one[k]) + radial * normal[k] for k in range(3)]
+
+
+def scatter_to(acc_ref, force, high, low):
+    group_ids = lax.broadcasted_iota(jnp.int32, (8, 128), 0)
+    lane_ids = lax.broadcasted_iota(jnp.int32, (128, 128), 0)
+    split = [p for f in force for p in pieces(f, 3)]
+    left, right = [], []
+    for k in range(8):
+        hit = jnp.broadcast_to(high[k : k + 1], (8, 128)) == group_ids
+        left.append(
+            jnp.concatenate(
+                [jnp.where(hit, jnp.broadcast_to(p[k : k + 1], (8, 128)), 0.0) for p in split], axis=0
+            ).astype(BF16)
+        )
+        same = jnp.broadcast_to(low[k : k + 1], (128, 128)) == lane_ids
+        right.append(jnp.where(same, 1.0, 0.0).astype(BF16))
+    acc_ref[...] += lax.dot_general(
+        jnp.concatenate(left, axis=1),
+        jnp.concatenate(right, axis=1),
+        (((1,), (1,)), ((), ())),
+        preferred_element_type=F32,
+    )
+
+
 def induce(
-    pos_ref, vel_ref, app_ref, sus_ref, own_ref, part_ref,
-    mom_ref, pos_cols, vel_cols, mom_cols, own_back, part_back,
+    pos_ref, vel_ref, app_ref, sus_ref, raw_ref, part_ref, count_ref,
+    mom_ref, force_ref,
+    pos_cols, vel_cols, mom_cols, own_ref, own_back, part_back, geo_ref, near_ref, far_ref, sums_ref,
     block_ref, block_all, first_ref, first_all, second_ref, rows_ref, weights_ref, target_ref, acc_ref, heads, tails,
     row_send, row_recv, one_send, one_recv, col_send, col_recv, two_send, two_recv, local_sem,
 ):
@@ -169,6 +220,17 @@
     target_ref[...] = target_rows(pos)
     acc_ref[...] = jnp.zeros_like(acc_ref)
     kept = (heads, tails)
+    sums_ref[...] = jnp.zeros_like(sums_ref)
+    columns, slots = raw_ref.shape
+    on_diagonal = lax.broadcasted_iota(jnp.int32, (columns, columns), 0) == lax.broadcasted_iota(
+        jnp.int32, (columns, columns), 1
+    )
+    counts = jnp.sum(
+        jnp.where(on_diagonal, jnp.broadcast_to(count_ref[...], (columns, columns)).astype(F32), 0.0),
+        axis=1, keepdims=True,
+    )
+    slot_ids = lax.broadcasted_iota(jnp.int32, (columns, slots), 1).astype(F32)
+    own_ref[...] = jnp.where(slot_ids < counts, raw_ref[...], -1)
 
     def row_copy(source, gathered, send, recv, step):
         to = row_steps(step)[0]
@@ -268,6 +330,45 @@
     acc_ref[...] = jnp.zeros_like(acc_ref)
     each_step("row", lambda step: row_copy(*one_args, step).start())
 
+    chunks = slots // 128
+    units = columns // 8 * chunks
+    groups = [slice(g * 128, g * 128 + 128) for g in range(length // 128)]
+    split_at = len(groups) // 2
+
+    def lists(unit):
+        eight = pl.ds(pl.multiple_of(lax.div(unit, chunks) * 8, 8), 8)
+        at = pl.ds(pl.multiple_of(lax.rem(unit, chunks) * 128, 128), 128)
+        here_own, here_part = own_ref[eight, at], part_ref[eight, at]
+        back_own, back_part = own_back[eight, at], part_back[eight, at]
+        return eight, ((here_own, here_part, here_own >= 0), (back_part, back_own, back_own >= 0))
+
+    def spread(ref, j):
+        return [jnp.broadcast_to(ref[j : j + 1, g], (8, 128)) for g in groups]
+
+    def halves(part, j, eight):
+        return [mom_cols[part, j, eight, groups[g]] for g in range(split_at)]
+
+    def col_done(step):
+        to, origin = col_steps(step)
+        for copy in col_copies(to, origin, step):
+            copy.wait()
+
+    each_step("col", col_done)
+    for copy in own_copies():
+        copy.wait()
+
+    @pl.loop(0, units)
+    def _(unit):
+        eight, both = lists(unit)
+        for which, (my_ids, other_ids, live) in enumerate(both):
+            mine, other = [], []
+            for near, far in ((pos_ref, pos_cols), (vel_ref, vel_cols)):
+                for j in range(3):
+                    mine.append(picked(spread(near, j), my_ids >> 7, my_ids & 127))
+                    other.append(picked([far[j, eight, g] for g in groups], other_ids >> 7, other_ids & 127))
+            for k, value in enumerate(geometry(mine, other, live)):
+                geo_ref[unit, which, k] = value
+
     def finish(part):
         at = slice(part * half, part * half + half)
         field = combine(acc_ref[:, at], pos_ref[:, at] - CENTRE)
@@ -313,107 +414,42 @@
     each_step("row", row_done)
     two_start(1)
 
-    def col_done(step):
-        to, origin = col_steps(step)
-        for copy in col_copies(to, origin, step):
-            copy.wait()
-
-    each_step("col", col_done)
-    for copy in own_copies():
-        copy.wait()
-    for part in range(2):
+
+    def two_done(part):
         each_step("col", lambda step: two_copy(part, *col_steps(step), step).wait())
         two_own(part).wait()
 
-
-def picked(table, high, low):
-    out = None
-    for group, row in enumerate(table):
-        found = jnp.take_along_axis(row, low, axis=1)
-        out = found if out is None else jnp.where(high == group, found, out)
-    return out
-
-
-def pair_force(mine, other):
-    sep = [mine[k] - other[k] for k in range(3)]
-    vel = [mine[3 + k] - other[3 + k] for k in range(3)]
-    m_one = mine[6:9]
-    m_two = other[6:9]
-
-    def dot(a, b):
-        return a[0] * b[0] + a[1] * b[1] + a[2] * b[2]
-
-    radius_sq = dot(sep, sep) + 1.0
-    inverse = lax.rsqrt(radius_sq)
-    distance = radius_sq * inverse
-    normal = [s * inverse for s in sep]
-    one = dot(m_one, normal)
-    two = dot(m_two, normal)
-    radial = 3.0 * (dot(m_one, m_two) - 5.0 * one * two)
-    radial = radial - 0.03 * (distance - 1.0) - 0.5 * dot(vel, normal)
-    return [3.0 * (one * m_two[k] + two * m_one[k]) + radial * normal[k] for k in range(3)]
-
-
-def contact_kernel(
-    pos_ref, vel_ref, mom_ref, pos_cols, vel_cols, mom_cols, own_ref, part_ref, own_back, part_back, out_ref, acc_ref
-):
-    columns = pos_cols.shape[1]
-    length = pos_ref.shape[1]
-    half = length // 2
-    chunks = own_ref.shape[1] // 128
-    acc_ref[...] = jnp.zeros_like(acc_ref)
-    group_ids = lax.broadcasted_iota(jnp.int32, (8, 128), 0)
-    lane_ids = lax.broadcasted_iota(jnp.int32, (128, 128), 0)
-    groups = [slice(g * 128, g * 128 + 128) for g in range(length // 128)]
-
-    def slots(my_ids, other_ids, live, eight):
-        my_high, my_low = my_ids >> 7, my_ids & 127
-        other_high, other_low = other_ids >> 7, other_ids & 127
-        mine, other = [], []
-        for k in range(9):
-            if k < 6:
-                near, far = (pos_ref, pos_cols) if k < 3 else (vel_ref, vel_cols)
-                j = k % 3
-                theirs = [far[j, eight, g] for g in groups]
-            else:
-                near, j = mom_ref, k - 6
-                theirs = [mom_cols[g.start // half, j, eight, g.start % half : g.start % half + 128] for g in groups]
-            ours = [jnp.broadcast_to(near[j : j + 1, g], (8, 128)) for g in groups]
-            mine.append(picked(ours, my_high, my_low))
-            other.append(picked(theirs, other_high, other_low))
-        force = [jnp.where(live, f, 0.0) for f in pair_force(mine, other)]
-        split = [p for f in force for p in pieces(f, 3)]
-        left, right = [], []
-        for k in range(8):
-            hit = jnp.broadcast_to(my_high[k : k + 1], (8, 128)) == group_ids
-            left.append(
-                jnp.concatenate(
-                    [jnp.where(hit, jnp.broadcast_to(p[k : k + 1], (8, 128)), 0.0) for p in split], axis=0
-                ).astype(BF16)
-            )
-            same = jnp.broadcast_to(my_low[k : k + 1], (128, 128)) == lane_ids
-            right.append(jnp.where(same, 1.0, 0.0).astype(BF16))
-        acc_ref[...] += lax.dot_general(
-            jnp.concatenate(left, axis=1),
-            jnp.concatenate(right, axis=1),
-            (((1,), (1,)), ((), ())),
-            preferred_element_type=F32,
-        )
-
-    @pl.loop(0, columns // 8 * chunks)
+    two_done(0)
+
+    @pl.loop(0, units)
     def _(unit):
-        eight = pl.ds(pl.multiple_of(lax.div(unit, chunks) * 8, 8), 8)
-        at = pl.ds(pl.multiple_of(lax.rem(unit, chunks) * 128, 128), 128)
-        owner, partner = own_ref[eight, at], part_ref[eight, at]
-        slots(owner, partner, owner >= 0, eight)
-        owner, partner = own_back[eight, at], part_back[eight, at]
-        slots(partner, owner, owner >= 0, eight)
+        eight, both = lists(unit)
+        for which, (my_ids, other_ids, live) in enumerate(both):
+            for j in range(3):
+                near_ref[unit, which, j] = picked(spread(mom_ref, j), my_ids >> 7, my_ids & 127)
+                far_ref[unit, which, j] = picked(halves(0, j, eight), other_ids >> 7, other_ids & 127)
+
+    two_done(1)
+
+    @pl.loop(0, units)
+    def _(unit):
+        eight, both = lists(unit)
+        for which, (my_ids, other_ids, live) in enumerate(both):
+            high, low = other_ids >> 7, other_ids & 127
+            theirs = [
+                jnp.where(high < split_at, far_ref[unit, which, j], picked(halves(1, j, eight), high, low, split_at))
+                for j in range(3)
+            ]
+            ours = [near_ref[unit, which, j] for j in range(3)]
+            normal = [geo_ref[unit, which, k] for k in range(3)]
+            force = pair_force(normal, geo_ref[unit, which, 3], ours, theirs)
+            scatter_to(sums_ref, force, my_ids >> 7, my_ids & 127)
 
     for k in range(3):
         base = 24 * k
-        total = acc_ref[base : base + 8] + (acc_ref[base + 8 : base + 16] + acc_ref[base + 16 : base + 24])
+        total = sums_ref[base : base + 8] + (sums_ref[base + 8 : base + 16] + sums_ref[base + 16 : base + 24])
         for g in range(8):
-            out_ref[k : k + 1, g * 128 : g * 128 + 128] = total[g : g + 1]
+            force_ref[k : k + 1, groups[g]] = total[g : g + 1]
 
 
 def on_device(positions, velocity, applied, suscept, contact_owner, contact_partner, contact_count):
@@ -421,25 +457,25 @@
     cols = lax.axis_size("col")
     length = positions.shape[1]
     slots = contact_owner.shape[3]
-    live = jnp.arange(slots, dtype=jnp.int32)[None, :] < contact_count.reshape(cols, 1)
-    owners = jnp.where(live, contact_owner.reshape(cols, slots), -1)
-    partners = contact_partner.reshape(cols, slots)
     copies = pltpu.SemaphoreType.DMA
     vector = jax.ShapeDtypeStruct((3, length), F32)
-    per_column = jax.ShapeDtypeStruct((3, cols, length), F32)
-    moments, pos_cols, vel_cols, mom_cols, own_back, part_back = pl.pallas_call(
+    units = cols // 8 * (slots // 128)
+    return pl.pallas_call(
         induce,
-        out_shape=(
-            vector,
-            per_column,
-            per_column,
-            jax.ShapeDtypeStruct((2, 3, cols, length // 2), F32),
-            jax.ShapeDtypeStruct((cols, slots), jnp.int32),
-            jax.ShapeDtypeStruct((cols, slots), jnp.int32),
-        ),
-        in_specs=vmem_specs(6),
-        out_specs=tuple(vmem_specs(6)),
+        out_shape=(vector, vector),
+        in_specs=vmem_specs(7),
+        out_specs=tuple(vmem_specs(2)),
         scratch_shapes=[
+            pltpu.VMEM((3, cols, length), F32),
+            pltpu.VMEM((3, cols, length), F32),
+            pltpu.VMEM((2, 3, cols, length // 2), F32),
+            pltpu.VMEM((cols, slots), jnp.int32),
+            pltpu.VMEM((cols, slots), jnp.int32),
+            pltpu.VMEM((cols, slots), jnp.int32),
+            pltpu.VMEM((units, 2, 4, 8, 128), F32),
+            pltpu.VMEM((units, 2, 3, 8, 128), F32),
+            pltpu.VMEM((units, 2, 3, 8, 128), F32),
+            pltpu.VMEM((72, 128), F32),
             pltpu.VMEM((6, length), F32),
             pltpu.VMEM((rows, 6, length), F32),
             pltpu.VMEM((3, length), F32),
@@ -459,16 +495,10 @@
             collective_id=0, has_side_effects=True, vmem_limit_bytes=67043328
         ),
         name="induce",
-    )(positions, velocity, applied, suscept.reshape(1, length), owners, partners)
-    forces = pl.pallas_call(
-        contact_kernel,
-        out_shape=vector,
-        in_specs=vmem_specs(10),
-        out_specs=pl.BlockSpec(memory_space=pltpu.VMEM),
-        scratch_shapes=[pltpu.VMEM((72, 128), F32)],
-        name="contacts",
-    )(positions, velocity, moments, pos_cols, vel_cols, mom_cols, owners, partners, own_back, part_back)
-    return (moments, forces)
+    )(
+        positions, velocity, applied, suscept.reshape(1, length),
+        contact_owner.reshape(cols, slots), contact_partner.reshape(cols, slots), contact_count.reshape(1, cols),
+    )
 
 
 def solution(mesh):

time: 78.8 us -> 74.5 us (0.945)
  Pallas kernels: 75.2 us -> 71.2 us
  other arithmetic: 1.44 us -> 0 us
    pallas_call x2 -> x1, Pallas kernels: 75.2 us -> 71.2 us  [on_device(): pl.pallas_call(induce, out_shape=(vector, vector), in_specs=vmem_specs(7)...]
    select_n x1 -> x0, other arithmetic: 1.44 us -> none  [on_device(): owners = jnp.where(live, contact_owner.reshape(cols, slots), -1)]
    unnamed x5 -> x4, local copies, waits for them, and re-layouts: 1.26 us -> 1.94 us
where the time goes in v4:
time: 74.5 us; the launch traced here: 73.7 us
  Pallas kernels  71.2 us (96%)
  local copies, waits for them, and re-layouts  1.94 us (3%)
    pallas_call x1, Pallas kernels, on_device(): pl.pallas_call(induce, out_shape=(vector, vector), in_specs=vmem_specs(7)...  71.2 us
    unnamed x4, local copies, waits for them, and re-layouts  1.94 us

profile of v4, /device:TPU:1, one launch (start us, length us, event | category | flops | bytes accessed | tf_op | source)
XLA Modules:
  0.0 73.7 jit_solution(867521980608496761)
XLA Ops:
  0.6 71.2 %induce.1 = (f32[3,1024]{1,0:T(4,128)}, f32[3,1024]{1,0:T(4,128)}) custom-call(f32[3,1024]{1,0:T(4,128)} %pos_ref.1, f32[3,1024]{1,0:T(4,128)} %vel_ref.1, f32[3,1024]{1,0:T(4,128)} %app_ref.1, f32[1,1024]{1,0:T(1,128)} %bitcast.6, s32[16,512]{1,0:T(8,128)} %bitcast.4, s32[16,512]{1,0:T(8,128)} %bitcast.5, s32[1,16]{1,0:T(1,128)} %bitcast.7), custom_call_target="tpu_custom_call" | custom-call | tf_op jit(solution)/shard_map/induce/pallas_call | solution.py:463
  71.8 0.0 copy-start
  71.8 1.3 %copy.11 = f32[3,1024]{1,0:T(4,128)} copy(f32[3,1024]{1,0:T(4,128)} %get-tuple-element.4) | data formatting | bytes 24576
  73.1 0.0 copy-done
  73.1 0.6 copy.12
Async XLA Ops:
  71.8 1.3 %copy-start = (f32[3,1024]{1,0:T(4,128)S(1)}, f32[3,1024]{1,0:T(4,128)}, u32[]{:S(2)}) copy-start(f32[3,1024]{1,0:T(4,128)} %get-tuple-element.5) | copy-start | bytes 36868

commit v5 on v4

--- a/solution.py
+++ b/solution.py
@@ -14,6 +14,8 @@
 SRC_BLOCK = 512
 ROW_SHAPE = (2, 4, 2)
 KEPT = 14
+TAIL_ROWS = 32
+EARLY = 4
 TGT_BLOCK = 256
 
 
@@ -49,6 +51,11 @@
     lax.fori_loop(1, lax.axis_size(axis), lambda step, carry: (body(step), carry)[1], 0)
 
 
+def every_step(axis, body):
+    for step in range(1, lax.axis_size(axis)):
+        body(step)
+
+
 def enter():
     barrier = pltpu.get_barrier_semaphore()
 
@@ -58,8 +65,8 @@
     def signal_col(step):
         pl.semaphore_signal(barrier, inc=1, device_id={"col": col_steps(step)[0]}, device_id_type=MESH)
 
-    each_step("row", signal_row)
-    each_step("col", signal_col)
+    every_step("row", signal_row)
+    every_step("col", signal_col)
 
 
 def pieces(value, count):
@@ -114,15 +121,18 @@
     return 3.0 * radial - direct + mixed
 
 
+def span(start, size):
+    return pl.ds(start if isinstance(start, int) else pl.multiple_of(start, size), size)
+
+
 def add_sums(weights, head, tail, acc_ref, to):
-    acc_ref[:, to] += jnp.dot(weights, head, preferred_element_type=F32) + jnp.dot(
-        weights, tail, preferred_element_type=F32
-    )
+    acc_ref[:, to] += jnp.dot(weights, head, preferred_element_type=F32)
+    acc_ref[0:TAIL_ROWS, to] += jnp.dot(weights[0:TAIL_ROWS], tail, preferred_element_type=F32)
 
 
 def add_field(rows_ref, weights_ref, target_ref, acc_ref, first, count, targets, kept=None):
     for start in range(0, count, SRC_BLOCK):
-        at = pl.ds(pl.multiple_of(first + start, SRC_BLOCK), SRC_BLOCK)
+        at = span(first + start, SRC_BLOCK)
         rows = rows_ref[:, at]
         weights = weights_ref[:, at]
         for low in range(targets[0], targets[1], TGT_BLOCK):
@@ -142,7 +152,7 @@
 
 
 def add_kept(kept, weights_ref, acc_ref, first, count, targets):
-    at = pl.ds(pl.multiple_of(first, count), count)
+    at = span(first, count)
     weights = weights_ref[:, at]
     for low in range(targets[0], targets[1], TGT_BLOCK):
         to = slice(low, low + TGT_BLOCK)
@@ -199,6 +209,13 @@
     )
 
 
+def two_by_two(low, high, body):
+    @pl.loop(low // 2, high // 2)
+    def _(index):
+        body(2 * index)
+        body(2 * index + 1)
+
+
 def induce(
     pos_ref, vel_ref, app_ref, sus_ref, raw_ref, part_ref, count_ref,
     mom_ref, force_ref,
@@ -286,49 +303,56 @@
         return pltpu.make_async_copy(second_ref.at[part], mom_cols.at[part, :, column, :], local_sem.at[4 + part])
 
     def two_start(part):
-        each_step("col", lambda step: two_copy(part, col_steps(step)[0], column, step).start())
+        every_step("col", lambda step: two_copy(part, col_steps(step)[0], column, step).start())
         two_own(part).start()
 
     def prepare(step, pos, mom, with_rows):
-        at = pl.ds(pl.multiple_of(step * length, length), length)
+        at = span(step * length, length)
         if with_rows:
             rows_ref[:, at] = source_rows(pos)
         weights_ref[:, at] = source_weights(pos, mom)
 
     prepare(0, pos, start, True)
+    add_field(rows_ref, weights_ref, target_ref, acc_ref, 0, length, (0, half), kept)
     pl.semaphore_wait(pltpu.get_barrier_semaphore(), lax.axis_size("row") + lax.axis_size("col") - 2)
-    each_step("row", lambda step: row_copy(*row_args, step).start())
+    every_step("row", lambda step: row_copy(*row_args, step).start())
+
+    def wait_first(step):
+        row_arrival(*row_args, step).wait_recv()
 
     def take_first(step):
-        row_arrival(*row_args, step).wait_recv()
         origin = row_steps(step)[1]
         prepare(step, block_all[origin, 0:3, :], block_all[origin, 3:6, :], True)
 
-    @pl.loop(0, KEPT)
+    add_field(rows_ref, weights_ref, target_ref, acc_ref, 0, length, (half, length), kept)
+    wait_first(1)
+    take_first(1)
+
+    @pl.loop(1, KEPT)
     def _(step):
-        @pl.when(step > 0)
-        def _():
-            take_first(step)
-
         @pl.when(step == 4)
         def _():
             each_step("col", col_start)
             for copy in own_copies():
                 copy.start()
 
+        wait_first(step + 1)
         add_field(rows_ref, weights_ref, target_ref, acc_ref, step * length, length, (0, length), kept)
-
-    @pl.loop(KEPT, parts)
-    def _(step):
-        take_first(step)
+        take_first(step + 1)
+
+    for step in range(KEPT, parts):
+        if step + 1 < parts:
+            wait_first(step + 1)
         add_field(rows_ref, weights_ref, target_ref, acc_ref, step * length, length, (0, length))
+        if step + 1 < parts:
+            take_first(step + 1)
 
     field = combine(acc_ref[...], pos)
     first = sus_ref[...] * (app_ref[...] + (field + start))
     first_ref[...] = first
     prepare(0, pos, first, False)
     acc_ref[...] = jnp.zeros_like(acc_ref)
-    each_step("row", lambda step: row_copy(*one_args, step).start())
+    every_step("row", lambda step: row_copy(*one_args, step).start())
 
     chunks = slots // 128
     units = columns // 8 * chunks
@@ -357,8 +381,7 @@
     for copy in own_copies():
         copy.wait()
 
-    @pl.loop(0, units)
-    def _(unit):
+    def pair_geometry(unit):
         eight, both = lists(unit)
         for which, (my_ids, other_ids, live) in enumerate(both):
             mine, other = [], []
@@ -369,6 +392,8 @@
             for k, value in enumerate(geometry(mine, other, live)):
                 geo_ref[unit, which, k] = value
 
+    two_by_two(0, EARLY, pair_geometry)
+
     def finish(part):
         at = slice(part * half, part * half + half)
         field = combine(acc_ref[:, at], pos_ref[:, at] - CENTRE)
@@ -376,23 +401,25 @@
         second_ref[part] = second
         mom_ref[:, at] = second
 
+    def wait_second(step):
+        row_arrival(*one_args, step).wait_recv()
+
     def take_second(step):
-        row_arrival(*one_args, step).wait_recv()
         origin = row_steps(step)[1]
         prepare(step, block_all[origin, 0:3, :], first_all[origin], False)
 
     @pl.loop(0, KEPT)
     def _(step):
-        @pl.when(step > 0)
-        def _():
-            take_second(step)
-
+        wait_second(step + 1)
         add_kept(kept, weights_ref, acc_ref, step * length, length, (0, half))
-
-    @pl.loop(KEPT, parts)
-    def _(step):
-        take_second(step)
+        take_second(step + 1)
+
+    for step in range(KEPT, parts):
+        if step + 1 < parts:
+            wait_second(step + 1)
         add_field(rows_ref, weights_ref, target_ref, acc_ref, step * length, length, (0, half))
+        if step + 1 < parts:
+            take_second(step + 1)
 
     finish(0)
 
@@ -419,20 +446,20 @@
         each_step("col", lambda step: two_copy(part, *col_steps(step), step).wait())
         two_own(part).wait()
 
+    two_by_two(EARLY, units, pair_geometry)
     two_done(0)
 
-    @pl.loop(0, units)
-    def _(unit):
+    def own_moments(unit):
         eight, both = lists(unit)
         for which, (my_ids, other_ids, live) in enumerate(both):
             for j in range(3):
                 near_ref[unit, which, j] = picked(spread(mom_ref, j), my_ids >> 7, my_ids & 127)
                 far_ref[unit, which, j] = picked(halves(0, j, eight), other_ids >> 7, other_ids & 127)
 
+    two_by_two(0, units, own_moments)
     two_done(1)
 
-    @pl.loop(0, units)
-    def _(unit):
+    def slot_forces(unit):
         eight, both = lists(unit)
         for which, (my_ids, other_ids, live) in enumerate(both):
             high, low = other_ids >> 7, other_ids & 127
@@ -443,11 +470,14 @@
             ours = [near_ref[unit, which, j] for j in range(3)]
             normal = [geo_ref[unit, which, k] for k in range(3)]
             force = pair_force(normal, geo_ref[unit, which, 3], ours, theirs)
-            scatter_to(sums_ref, force, my_ids >> 7, my_ids & 127)
+            scatter_to(sums_ref.at[which], force, my_ids >> 7, my_ids & 127)
+
+    two_by_two(0, units, slot_forces)
+    totals = sums_ref[0] + sums_ref[1]
 
     for k in range(3):
         base = 24 * k
-        total = sums_ref[base : base + 8] + (sums_ref[base + 8 : base + 16] + sums_ref[base + 16 : base + 24])
+        total = totals[base : base + 8] + (totals[base + 8 : base + 16] + totals[base + 16 : base + 24])
         for g in range(8):
             force_ref[k : k + 1, groups[g]] = total[g : g + 1]
 
@@ -475,7 +505,7 @@
             pltpu.VMEM((units, 2, 4, 8, 128), F32),
             pltpu.VMEM((units, 2, 3, 8, 128), F32),
             pltpu.VMEM((units, 2, 3, 8, 128), F32),
-            pltpu.VMEM((72, 128), F32),
+            pltpu.VMEM((2, 72, 128), F32),
             pltpu.VMEM((6, length), F32),
             pltpu.VMEM((rows, 6, length), F32),
             pltpu.VMEM((3, length), F32),

time: 74.5 us -> 72.1 us (0.968)
  Pallas kernels: 71.2 us -> 69.3 us
    pallas_call x1, Pallas kernels: 71.2 us -> 69.3 us  [on_device(): pl.pallas_call(induce, out_shape=(vector, vector), in_specs=vmem_specs(7)...]
where the time goes in v5:
time: 72.1 us; the launch traced here: 71.9 us
  Pallas kernels  69.3 us (96%)
  local copies, waits for them, and re-layouts  1.94 us (3%)
    pallas_call x1, Pallas kernels, on_device(): pl.pallas_call(induce, out_shape=(vector, vector), in_specs=vmem_specs(7)...  69.3 us
    unnamed x4, local copies, waits for them, and re-layouts  1.94 us

profile of v5, /device:TPU:1, one launch (start us, length us, event | category | flops | bytes accessed | tf_op | source)
XLA Modules:
  0.0 71.9 jit_solution(4817006822626601710)
XLA Ops:
  0.6 69.3 %induce.1 = (f32[3,1024]{1,0:T(4,128)}, f32[3,1024]{1,0:T(4,128)}) custom-call(f32[3,1024]{1,0:T(4,128)} %pos_ref.1, f32[3,1024]{1,0:T(4,128)} %vel_ref.1, f32[3,1024]{1,0:T(4,128)} %app_ref.1, f32[1,1024]{1,0:T(1,128)} %bitcast.6, s32[16,512]{1,0:T(8,128)} %bitcast.4, s32[16,512]{1,0:T(8,128)} %bitcast.5, s32[1,16]{1,0:T(1,128)} %bitcast.7), custom_call_target="tpu_custom_call" | custom-call | tf_op jit(solution)/shard_map/induce/pallas_call | solution.py:493
  69.9 0.0 copy-start
  69.9 1.3 %copy.11 = f32[3,1024]{1,0:T(4,128)} copy(f32[3,1024]{1,0:T(4,128)} %get-tuple-element.4) | data formatting | bytes 24576
  71.3 0.0 copy-done
  71.3 0.6 copy.12
Async XLA Ops:
  69.9 1.3 %copy-start = (f32[3,1024]{1,0:T(4,128)S(1)}, f32[3,1024]{1,0:T(4,128)}, u32[]{:S(2)}) copy-start(f32[3,1024]{1,0:T(4,128)} %get-tuple-element.5) | copy-start | bytes 36868

commit v6 on v5

--- a/solution.py
+++ b/solution.py
@@ -13,6 +13,7 @@
 CENTRE = 8.0
 SRC_BLOCK = 512
 ROW_SHAPE = (2, 4, 2)
+COL_SHAPE = (4, 4)
 KEPT = 14
 TAIL_ROWS = 32
 EARLY = 4
@@ -42,9 +43,28 @@
 
 
 def col_steps(step):
-    size = lax.axis_size("col")
+    wide, deep = COL_SHAPE
     me = lax.axis_index("col")
-    return lax.rem(me + step, size), lax.rem(me + size - step, size)
+    x, z = lax.div(me, deep), lax.rem(me, deep)
+    if isinstance(step, int):
+        x_by, z_by = step // deep, step % deep
+    else:
+        x_by, z_by = lax.div(step, deep), lax.rem(step, deep)
+
+    def at(sign):
+        return lax.rem(x + wide + sign * x_by, wide) * deep + lax.rem(z + deep + sign * z_by, deep)
+
+    return at(1), at(-1)
+
+
+def far_first():
+    wide, deep = COL_SHAPE
+
+    def hops(step):
+        x_by, z_by = step // deep, step % deep
+        return 2 * min(z_by, deep - z_by) + min(x_by, wide - x_by)
+
+    return sorted(range(1, wide * deep), key=hops, reverse=True)
 
 
 def each_step(axis, body):
@@ -218,7 +238,7 @@
 
 def induce(
     pos_ref, vel_ref, app_ref, sus_ref, raw_ref, part_ref, count_ref,
-    mom_ref, force_ref,
+    both_ref,
     pos_cols, vel_cols, mom_cols, own_ref, own_back, part_back, geo_ref, near_ref, far_ref, sums_ref,
     block_ref, block_all, first_ref, first_all, second_ref, rows_ref, weights_ref, target_ref, acc_ref, heads, tails,
     row_send, row_recv, one_send, one_recv, col_send, col_recv, two_send, two_recv, local_sem,
@@ -229,6 +249,7 @@
     here = lax.axis_index("row")
     column = lax.axis_index("col")
 
+    mom_ref, force_ref = both_ref.at[0], both_ref.at[1]
     enter()
     pos = pos_ref[...] - CENTRE
     start = sus_ref[...] * app_ref[...]
@@ -303,7 +324,8 @@
         return pltpu.make_async_copy(second_ref.at[part], mom_cols.at[part, :, column, :], local_sem.at[4 + part])
 
     def two_start(part):
-        every_step("col", lambda step: two_copy(part, col_steps(step)[0], column, step).start())
+        for step in far_first():
+            two_copy(part, col_steps(step)[0], column, step).start()
         two_own(part).start()
 
     def prepare(step, pos, mom, with_rows):
@@ -434,12 +456,9 @@
     add_field(rows_ref, weights_ref, target_ref, acc_ref, KEPT * length, (parts - KEPT) * length, (half, length))
     finish(1)
 
-    def row_done(step):
-        row_copy(*row_args, step).wait_send()
-        row_copy(*one_args, step).wait_send()
-
-    each_step("row", row_done)
+    each_step("row", lambda step: row_copy(*row_args, step).wait_send())
     two_start(1)
+    each_step("row", lambda step: row_copy(*one_args, step).wait_send())
 
 
     def two_done(part):
@@ -488,13 +507,12 @@
     length = positions.shape[1]
     slots = contact_owner.shape[3]
     copies = pltpu.SemaphoreType.DMA
-    vector = jax.ShapeDtypeStruct((3, length), F32)
     units = cols // 8 * (slots // 128)
-    return pl.pallas_call(
+    both = pl.pallas_call(
         induce,
-        out_shape=(vector, vector),
+        out_shape=jax.ShapeDtypeStruct((2, 3, length), F32),
         in_specs=vmem_specs(7),
-        out_specs=tuple(vmem_specs(2)),
+        out_specs=pl.BlockSpec(memory_space=pltpu.VMEM),
         scratch_shapes=[
             pltpu.VMEM((3, cols, length), F32),
             pltpu.VMEM((3, cols, length), F32),
@@ -529,6 +547,7 @@
         positions, velocity, applied, suscept.reshape(1, length),
         contact_owner.reshape(cols, slots), contact_partner.reshape(cols, slots), contact_count.reshape(1, cols),
     )
+    return (both[0], both[1])
 
 
 def solution(mesh):

time: 72.1 us -> 71.4 us (level)
    unnamed x4 -> x0, local copies, waits for them, and re-layouts: 1.94 us -> none
    squeeze x0 -> x1, local copies, waits for them, and re-layouts: none -> 1.35 us  [on_device(): return (both[0], both[1])]
where the time goes in v6:
time: 71.4 us; the launch traced here: 71.1 us
  Pallas kernels  69.1 us (97%)
  local copies, waits for them, and re-layouts  1.35 us (2%)
    pallas_call x1, Pallas kernels, on_device(): pl.pallas_call(induce, out_shape=jax.ShapeDtypeStruct((2, 3, length), F32...  69.1 us

profile of v6, /device:TPU:1, one launch (start us, length us, event | category | flops | bytes accessed | tf_op | source)
XLA Modules:
  0.0 71.1 jit_solution(7569162102641777583)
XLA Ops:
  0.6 69.1 %induce.1 = f32[2,3,1024]{2,1,0:T(4,128)} custom-call(f32[3,1024]{1,0:T(4,128)} %pos_ref.1, f32[3,1024]{1,0:T(4,128)} %vel_ref.1, f32[3,1024]{1,0:T(4,128)} %app_ref.1, f32[1,1024]{1,0:T(1,128)} %bitcast.10, s32[16,512]{1,0:T(8,128)} %bitcast.8, s32[16,512]{1,0:T(8,128)} %bitcast.9, s32[1,16]{1,0:T(1,128)} %bitcast.11), custom_call_target="tpu_custom_call" | custom-call | tf_op jit(solution)/shard_map/induce/pallas_call | solution.py:511
  69.8 1.4 %slice_bitcast_fusion = (f32[3,1024]{1,0:T(4,128)}, f32[3,1024]{1,0:T(4,128)}) fusion(f32[2,3,1024]{2,1,0:T(4,128)} %induce.1), kind=kLoop, calls=%fused_computation | loop fusion | bytes 49152 | tf_op jit(solution)/shard_map/squeeze | solution.py:550
